TPU v7x, 128 devices: a whole 4x4x4 slice. The times are simulated.
128 devices in a mesh: row: 8 (over z, y_hi), col: 16 (over y_lo, x, core).
Axes of the slice: x: 4, y: 4 (y_hi: 2, y_lo: 2; y = y_hi * 2 + y_lo), z: 4, core: 2. Of those that a mesh axis runs over, the one named last changes fastest.
Arguments:
- ancestor: float32 [16384, 16384], P('row', 'col'), may hold values from -6 to 6
- factor: float32 [2, 16384, 512], P(None, ('row', 'col')), may hold values from -0.0625 to 0.0625
- diag_inverse: float32 [2, 512, 512], replicated, may hold values from -6 to 6
- structure: int32 [2, 16], replicated, may hold values from 0 to 31, as said below
Outputs:
- off_diagonal: float32 [2, 16384, 512], P(None, ('row', 'col'))
- diag_block: float32 [2, 512, 512], replicated
Inputs may be any that keep to these rules, and one draw needn't show every extreme that they name: `structure`: each row holds 16 distinct tile indices; tile t covers rows t * 512 to t * 512 + 511.
All inputs are finite; a program needn't handle non-finite values.
Results may differ from a plain program's by a relative error of at most 0.0001.
Values sent between devices are 32-bit elements; how exact they have to be, the bound alone decides.
No kernel may reach another device: no remote copies, remote signals or barrier semaphores. Data moves between devices by JAX's collectives and lax.ppermute only.
A program may use at most 128 MiB of HBM per device.

v0:
```python
import jax
import jax.numpy as jnp
from jax import lax
from jax.experimental import pallas as pl
from jax.experimental.pallas import tpu as pltpu
from jax.sharding import Mesh
from jax.sharding import PartitionSpec as P

TILE = 512
WIDTH = 512

ROW, COL = ("z", "yh"), ("yl", "x", "core")
AXES, CHIPS = ROW + COL, ROW + COL[:2]


def route(move):
    pairs = []
    for d in range(128):
        z, yh, yl, x, core = d // 32, d // 16 % 2, d // 8 % 2, d // 2 % 4, d % 2
        z, y, x, core = move(z, yh * 2 + yl, x, core)
        z, y, x = z % 4, y % 4, x % 4
        pairs.append((d, z * 32 + (y // 2) * 16 + (y % 2) * 8 + x * 2 + core))
    return pairs


def to_core(v):
    return lax.ppermute(v, AXES, route(lambda z, y, x, c: (z, y, x, 1 - c)))


def to_x(v, s):
    return lax.ppermute(v, AXES, route(lambda z, y, x, c: (z, y, x + s, c)))


def to_y(v, s):
    return lax.ppermute(v, AXES, route(lambda z, y, x, c: (z, y + s, x, c)))


def to_yl(v):
    return lax.ppermute(v, AXES, route(lambda z, y, x, c: (z, y ^ 1, x, c)))


def to_z(v, s):
    return lax.ppermute(v, AXES, route(lambda z, y, x, c: (z + s, y, x, c)))


def halves(a):
    hi = a.astype(jnp.bfloat16)
    return hi, (a - hi.astype(jnp.float32)).astype(jnp.bfloat16)


def panel_kernel(info, own, oth, f0, f1, f2, f3, g_own, g_oth, *rest):
    outs, (f_hi, f_lo, acc) = rest[:6], rest[6:]
    i = pl.program_id(0)
    core, z, yh, x, yl = info[8], info[9], info[10], info[11], info[12]

    @pl.when(i == 0)
    def _():
        def place(value, col, row):
            at = pl.ds(pl.multiple_of(col * 128 + row * 16, 16), 16)
            hi, lo = halves(value)
            f_hi[at, :] = hi
            f_lo[at, :] = lo

        for s, ref in enumerate((f0, f1, f2, f3)):
            from_z = lax.rem(z + 4 - s, 4)

            @pl.loop(0, 8)
            def _(col):
                for h in range(2):
                    place(ref[h, col], col, from_z * 2 + h)

        for ref, from_yh in ((g_own, yh), (g_oth, 1 - yh)):
            for s in range(4):
                from_z = lax.rem(z + 4 - s, 4)

                @pl.loop(0, 8)
                def _(col):
                    place(ref[s, col], col + 8, from_z * 2 + from_yh)

    acc[...] = jnp.zeros_like(acc)
    for ref, side in ((own, core), (oth, 1 - core)):
        for j in range(2):
            tile = side * 2 + j

            @pl.when((info[i] > 0) & (info[4 + tile] > 0))
            def _():
                at = pl.ds(pl.multiple_of(tile * TILE, TILE), TILE)
                hi, lo = halves(ref[:, j * TILE : (j + 1) * TILE])
                b_hi = f_hi[at, :]
                acc[...] += (
                    jnp.dot(hi, b_hi, preferred_element_type=jnp.float32)
                    + jnp.dot(lo, b_hi, preferred_element_type=jnp.float32)
                    + jnp.dot(hi, f_lo[at, :], preferred_element_type=jnp.float32)
                )

    to_l = lax.div(i, 2)
    for b in range(2):
        step = lax.rem(lax.rem(i, 2) * 2 + b + 4 - x, 4)
        first = acc[b * 256 : b * 256 + 128, :]
        last = acc[b * 256 + 128 : b * 256 + 256, :]
        for s in range(4):

            @pl.when(step == s)
            def _():
                outs[s][to_l] = first

        @pl.when(to_l == yl)
        def _():
            outs[4][step] = last

        @pl.when(to_l != yl)
        def _():
            outs[5][step] = last


def panel(info, own, oth, pieces):
    cols = pieces[0].shape[-1]
    whole = lambda v: pl.BlockSpec(v.shape, lambda i, info: (0,) * len(v.shape))
    block = pl.BlockSpec((TILE, own.shape[1]), lambda i, info: (info[13 + i], 0))
    out = [jax.ShapeDtypeStruct((2, 128, cols), jnp.float32)] * 4
    out += [jax.ShapeDtypeStruct((4, 128, cols), jnp.float32)] * 2
    return pl.pallas_call(
        panel_kernel,
        grid_spec=pltpu.PrefetchScalarGridSpec(
            num_scalar_prefetch=1,
            grid=(4,),
            in_specs=[block, block] + [whole(v) for v in pieces],
            out_specs=[whole(v) for v in out],
            scratch_shapes=[
                pltpu.VMEM((2048, cols), jnp.bfloat16),
                pltpu.VMEM((2048, cols), jnp.bfloat16),
                pltpu.VMEM((TILE, cols), jnp.float32),
            ],
        ),
        out_shape=out,
        compiler_params=pltpu.CompilerParams(vmem_limit_bytes=44 << 20),
        cost_estimate=pl.CostEstimate(
            flops=3 * 2 * 2048 * 2048 * cols,
            bytes_accessed=20 << 20,
            transcendentals=0,
        ),
    )(info, own, oth, *pieces)


def product(left, right):
    return lax.dot_general(
        left,
        right,
        (((0,), (0,)), ((), ())),
        precision=lax.Precision.HIGH,
        preferred_element_type=jnp.float32,
    )


def pick(v, i):
    return lax.dynamic_index_in_dim(v, i, 0, keepdims=False)


def per_device(ancestor, factor, diag_inverse, structure):
    z, yh, yl, x, core = (lax.axis_index(axis) for axis in AXES)
    row, group = z * 2 + yh, yl * 4 + x
    at_first = core == 0
    half = WIDTH // 2

    f_keep = pick(factor, core)
    f_got = to_core(pick(factor, 1 - core))

    spread = lax.all_to_all(factor.reshape(2, 8, 16, WIDTH), ROW, 1, 0)
    spread = lax.all_to_all(spread.reshape(16, 16, WIDTH), COL, 0, 0)
    spread, ancestor, f_got = lax.optimization_barrier((spread, ancestor, f_got))
    oth = to_core(ancestor)
    low, high = spread[:8], spread[8:]
    low_y, *high_z = lax.optimization_barrier(
        (to_y(low, 2), high, *(to_z(high, s) for s in (1, 2, 3)))
    )
    f_first = jnp.where(at_first, f_keep, f_got)
    f_last = jnp.where(at_first, f_got, f_keep)
    pair = jnp.where(yh == 0, jnp.stack([low, low_y]), jnp.stack([low_y, low]))
    quad = jnp.stack(high_z)

    listed = pick(structure, core)
    four = jnp.arange(4, dtype=jnp.int32)
    flag = lambda tiles: jnp.any(listed[None, :] == tiles[:, None], axis=1)
    rows_on = flag(row * 4 + four)
    past = jnp.where(rows_on[None, :] & (four[None, :] <= four[:, None]), four[None, :], 0)
    info = jnp.concatenate(
        [
            rows_on.astype(jnp.int32),
            flag(group * 4 + four).astype(jnp.int32),
            jnp.stack([core, z, yh, x, yl]).astype(jnp.int32),
            jnp.max(past, axis=1),
        ]
    )

    gathered = []
    for c in range(2):
        cut = lambda v: v[..., c * half : (c + 1) * half]
        pairs = [cut(pair)] + [to_z(cut(pair), s) for s in (1, 2, 3)]
        gathered.append([*pairs, cut(quad), to_y(cut(quad), 2)])
    fy = to_yl(f_first)
    fx = [to_x(f_last, s) for s in (3, 2, 1)]
    f_firsts = jnp.where(yl == 0, jnp.stack([f_first, fy]), jnp.stack([fy, f_first]))
    f_lasts = jnp.stack([f_last, *fx])

    firsts, lasts, diags = [], [], []
    for c in range(2):
        first0, first1, first2, first3, last_keep, last_send = panel(
            info, ancestor, oth, gathered[c]
        )
        last_got = to_yl(last_send)
        got = [to_x(first1, 1), to_x(first3, 3), to_x(first2, 2)]
        first = first0 + got[0] + got[1] + got[2]
        last = last_keep + last_got
        firsts.append(first)
        lasts.append(last)
        diags.append(
            product(f_firsts.reshape(256, WIDTH), first.reshape(256, half))
            + product(f_lasts.reshape(512, WIDTH), last.reshape(512, half))
        )

    diag = jnp.concatenate(diags, axis=1)
    diag = lax.all_to_all(diag.reshape(64, 8, WIDTH), CHIPS, 0, 0)
    diag = jnp.sum(diag, axis=0)
    diag = jnp.broadcast_to(diag, (64, 8, WIDTH))
    diag = lax.all_to_all(diag, CHIPS, 0, 0).reshape(WIDTH, WIDTH)
    diag_oth = to_core(diag)
    both = jnp.where(
        at_first, jnp.stack([diag, diag_oth]), jnp.stack([diag_oth, diag])
    )

    first = jnp.stack(firsts, axis=1)
    last = jnp.stack(lasts, axis=1)
    first = pick(first, yl) + to_yl(pick(first, 1 - yl))
    last = last[0] + to_x(last[1], 1) + to_x(last[3], 3) + to_x(last[2], 2)
    mine = jnp.where(at_first, first, last)
    theirs = to_core(jnp.where(at_first, last, first))
    off = -jnp.where(at_first, jnp.stack([mine, theirs]), jnp.stack([theirs, mine]))
    off = jnp.concatenate([off[:, 0], off[:, 1]], axis=-1)
    return off, diag_inverse + both


def solution(mesh):
    mesh = Mesh(mesh.devices.reshape(4, 2, 2, 4, 2), AXES)
    in_specs = (P(ROW, COL), P(None, AXES, None), P(), P())
    out_specs = (P(None, AXES, None), P())

    return jax.shard_map(
        per_device, mesh=mesh, in_specs=in_specs, out_specs=out_specs, check_vma=False
    )
```

profile of v0, /device:TPU:1, one launch (start us, length us, event | category | flops | bytes accessed | tf_op | source)
XLA Modules:
  0.0 205.8 jit_solution(11879818109359141642)
XLA Ops:
  1.8 19.1 %all_to_all.30 = f32[1,2,8,16,512]{4,3,1,0,2:T(8,128)} all-to-all(f32[1,2,8,16,512]{4,3,1,0,2:T(8,128)S(1)} %copy.44), channel_id=1, replica_groups=mesh['z'=4,'yh'=2,'yl'=2,'x'=4,'core'=2] {'z','yh'}, dimensions={2} | all-to-all | bytes 1048576 | tf_op jit(solution)/shard_map/all_to_all | solution.py:168
  20.9 6.2 %all-to-all-start.1 = ((f32[16,16,512]{2,1,0:T(8,128)}), f32[16,16,512]{2,1,0:T(8,128)S(1)}, u32[]{:S(2)}, u32[]{:S(2)}) async-start(f32[16,16,512]{2,1,0:T(8,128)} %bitcast.9), calls=%async_computation.1 | async-start | bytes 1048576 | tf_op jit(solution)/shard_map/all_to_all | solution.py:169
  27.4 1.4 collective-permute-done
  28.8 7.8 %all-to-all-done.1 = f32[16,16,512]{2,1,0:T(8,128)S(1)} async-done(((f32[16,16,512]{2,1,0:T(8,128)}), f32[16,16,512]{2,1,0:T(8,128)S(1)}, u32[]{:S(2)}, u32[]{:S(2)}) %all-to-all-start.1) | async-done | bytes 524320 | tf_op jit(solution)/shard_map/all_to_all | solution.py:169
  36.6 1.4 collective-permute-start.1
  38.3 1.7 collective-permute-start.4
  42.4 7.2 %collective-permute-done.2 = f32[8,16,512]{2,1,0:T(8,128)S(1)} collective-permute-done((f32[8,16,512]{2,1,0:T(8,128)S(1)}, f32[8,16,512]{2,1,0:T(8,128)S(1)}, u32[]{:S(2)}, u32[]{:S(2)}) %collective-permute-start.2) | collective-permute-done | bytes 262176 | tf_op jit(solution)/shard_map/ppermute | solution.py:35
  49.7 3.3 %collective-permute-done.3 = f32[8,16,512]{2,1,0:T(8,128)S(1)} collective-permute-done((f32[8,16,512]{2,1,0:T(8,128)S(1)}, f32[8,16,512]{2,1,0:T(8,128)S(1)}, u32[]{:S(2)}, u32[]{:S(2)}) %collective-permute-start.3) | collective-permute-done | bytes 262176 | tf_op jit(solution)/shard_map/ppermute | solution.py:43
  55.6 3.1 %collective-permute-start.7 = (f32[2,8,16,256]{3,2,1,0:T(8,128)S(1)}, f32[2,8,16,256]{3,2,1,0:T(8,128)S(1)}, u32[]{:S(2)}, u32[]{:S(2)}) collective-permute-start(f32[2,8,16,256]{3,2,1,0:T(8,128)S(1)} %get-tuple-element.57.f0), channel_id=1, source_target_pairs={{0,64},{1,65},{2,66},{3,67},{4,68},{5,69},{6,70},{7,71},{8,72},{9,... | collective-permute-start | bytes 786440 | tf_op jit(solution)/shard_map/ppermute | solution.py:43
  59.0 1.7 bitcast_select_fusion.1
  60.7 1.9 collective-permute-done.6.f1
  63.3 6.5 %collective-permute-done.7.f2 = f32[2,8,16,256]{3,2,1,0:T(8,128)S(1)} collective-permute-done((f32[2,8,16,256]{3,2,1,0:T(8,128)S(1)}, f32[2,8,16,256]{3,2,1,0:T(8,128)S(1)}, u32[]{:S(2)}, u32[]{:S(2)}) %collective-permute-start.7) | collective-permute-done | bytes 262176 | tf_op jit(solution)/shard_map/ppermute | solution.py:43
  71.4 2.8 %collective-permute-start.15 = (f32[2,8,16,256]{3,2,1,0:T(8,128)S(1)}, f32[2,8,16,256]{3,2,1,0:T(8,128)S(1)}, u32[]{:S(2)}, u32[]{:S(2)}) collective-permute-start(f32[2,8,16,256]{3,2,1,0:T(8,128)S(1)} %get-tuple-element.56.f0), channel_id=1, source_target_pairs={{0,96},{1,97},{2,98},{3,99},{4,100},{5,101},{6,102},{7,103},{8,104... | collective-permute-start | bytes 786440 | tf_op jit(solution)/shard_map/ppermute | solution.py:43
  74.2 1.9 collective-permute-start.16
  79.0 9.7 %shard_map.59 = (f32[2,128,256]{2,1,0:T(8,128)S(1)}, f32[2,128,256]{2,1,0:T(8,128)}, f32[2,128,256]{2,1,0:T(8,128)S(1)}, f32[2,128,256]{2,1,0:T(8,128)S(1)}, f32...) custom-call(s32[17]{0:T(128)S(1)} %concatenate.9.info, f32[2048,1024]{1,0:T(8,128)} %own.1, ...), custom_call_target="tpu_custom_call" | custom-call | flops 6442450944 | bytes 20971520 | tf_op jit(solution)/shard_map/pallas_call | solution.py:122
  90.3 9.9 %shard_map.60 = (f32[2,128,256]{2,1,0:T(8,128)S(1)}, f32[2,128,256]{2,1,0:T(8,128)}, f32[2,128,256]{2,1,0:T(8,128)}, f32[2,128,256]{2,1,0:T(8,128)}, f32[4,128,2...) custom-call(s32[17]{0:T(128)S(1)} %concatenate.9.info, f32[2048,1024]{1,0:T(8,128)} %own.1, ...), custom_call_target="tpu_custom_call" | custom-call | flops 6442450944 | bytes 20971520 | tf_op jit(solution)/shard_map/pallas_call | solution.py:122
  100.2 2.2 %collective-permute-start.19 = (f32[2,128,256]{2,1,0:T(8,128)}, f32[2,128,256]{2,1,0:T(8,128)S(1)}, u32[]{:S(2)}, u32[]{:S(2)}) collective-permute-start(f32[2,128,256]{2,1,0:T(8,128)} %get-tuple-element.36), channel_id=1, source_target_pairs={{0,4},{1,5},{2,6},{3,7},{4,0},{5,1},{6,2},{7,3},{8,12},{9,13},{10,... | collective-permute-start | bytes 786440 | tf_op jit(solution)/shard_map/ppermute | solution.py:31
  102.4 2.1 %collective-permute-start.22 = (f32[4,128,256]{2,1,0:T(8,128)S(1)}, f32[4,128,256]{2,1,0:T(8,128)}, u32[]{:S(2)}, u32[]{:S(2)}) collective-permute-start(f32[4,128,256]{2,1,0:T(8,128)S(1)} %get-tuple-element.40), channel_id=1, source_target_pairs={{0,8},{1,9},{2,10},{3,11},{4,12},{5,13},{6,14},{7,15},{8,0},{9,1},... | collective-permute-start | bytes 1572872 | tf_op jit(solution)/shard_map/ppermute | solution.py:39
  107.8 2.2 %collective-permute-done.19 = f32[2,128,256]{2,1,0:T(8,128)S(1)} collective-permute-done((f32[2,128,256]{2,1,0:T(8,128)}, f32[2,128,256]{2,1,0:T(8,128)S(1)}, u32[]{:S(2)}, u32[]{:S(2)}) %collective-permute-start.19) | collective-permute-done | bytes 262176 | tf_op jit(solution)/shard_map/ppermute | solution.py:31
  112.5 2.1 %collective-permute-done.18 = f32[2,128,256]{2,1,0:T(8,128)} collective-permute-done((f32[2,128,256]{2,1,0:T(8,128)}, f32[2,128,256]{2,1,0:T(8,128)}, u32[]{:S(2)}, u32[]{:S(2)}) %collective-permute-start.18) | collective-permute-done | bytes 262176 | tf_op jit(solution)/shard_map/ppermute | solution.py:31
  114.6 3.5 %collective-permute-start.27 = (f32[128,512]{1,0:T(8,128)}, f32[128,512]{1,0:T(8,128)S(1)}, u32[]{:S(2)}, u32[]{:S(2)}) collective-permute-start(f32[128,512]{1,0:T(8,128)} %get-tuple-element.52), channel_id=1, source_target_pairs={{0,8},{1,9},{2,10},{3,11},{4,12},{5,13},{6,14},{7,15},{8,0},{9,1},... | collective-permute-start | bytes 786440 | tf_op jit(solution)/shard_map/ppermute | solution.py:39
  119.8 1.4 collective-permute-done.29
  121.2 4.6 %collective-permute-done.28 = f32[128,512]{1,0:T(8,128)S(1)} collective-permute-done((f32[128,512]{1,0:T(8,128)}, f32[128,512]{1,0:T(8,128)S(1)}, u32[]{:S(2)}, u32[]{:S(2)}) %collective-permute-start.28) | collective-permute-done | bytes 262176 | tf_op jit(solution)/shard_map/ppermute | solution.py:31
  125.8 1.7 convolution_bitcast_fusion
  127.9 7.5 %collective-permute-done.21 = f32[4,128,256]{2,1,0:T(8,128)S(1)} collective-permute-done((f32[4,128,256]{2,1,0:T(8,128)S(1)}, f32[4,128,256]{2,1,0:T(8,128)S(1)}, u32[]{:S(2)}, u32[]{:S(2)}) %collective-permute-start.21) | collective-permute-done | bytes 524320 | tf_op jit(solution)/shard_map/ppermute | solution.py:39
  138.1 11.7 %all-to-all-start.2 = ((f32[64,8,512]{2,1,0:T(8,128)}), f32[64,8,512]{2,1,0:T(8,128)S(1)}, u32[]{:S(2)}, u32[]{:S(2)}) async-start(f32[64,8,512]{2,1,0:T(8,128)} %bitcast.42), calls=%async_computation.2 | async-start | bytes 2097152 | tf_op jit(solution)/shard_map/all_to_all | solution.py:222
  149.7 18.2 %all-to-all-done.2 = f32[64,8,512]{2,1,0:T(8,128)S(1)} async-done(((f32[64,8,512]{2,1,0:T(8,128)}), f32[64,8,512]{2,1,0:T(8,128)S(1)}, u32[]{:S(2)}, u32[]{:S(2)}) %all-to-all-start.2) | async-done | bytes 1048608 | tf_op jit(solution)/shard_map/all_to_all | solution.py:222
  169.1 5.0 %all-to-all-start.3 = ((f32[64,8,512]{2,1,0:T(8,128)}), f32[64,8,512]{2,1,0:T(8,128)S(1)}, u32[]{:S(2)}, u32[]{:S(2)}) async-start(f32[64,8,512]{2,1,0:T(8,128)} %broadcast_in_dim.9), calls=%async_computation.3 | async-start | bytes 2097152 | tf_op jit(solution)/shard_map/all_to_all | solution.py:225
  179.2 2.7 %collective-permute-start.25 = (f32[2,128,256]{2,1,0:T(8,128)}, f32[2,128,256]{2,1,0:T(8,128)S(1)}, u32[]{:S(2)}, u32[]{:S(2)}) collective-permute-start(f32[2,128,256]{2,1,0:T(8,128)} %get-tuple-element.48), channel_id=1, source_target_pairs={{0,4},{1,5},{2,6},{3,7},{4,0},{5,1},{6,2},{7,3},{8,12},{9,13},{10,... | collective-permute-start | bytes 786440 | tf_op jit(solution)/shard_map/ppermute | solution.py:31
  183.3 8.0 %all-to-all-done.3 = f32[64,8,512]{2,1,0:T(8,128)S(1)} async-done(((f32[64,8,512]{2,1,0:T(8,128)}), f32[64,8,512]{2,1,0:T(8,128)S(1)}, u32[]{:S(2)}, u32[]{:S(2)}) %all-to-all-start.3) | async-done | bytes 1048608 | tf_op jit(solution)/shard_map/all_to_all | solution.py:225
  191.3 7.2 %collective-permute-start.31 = (f32[512,512]{1,0:T(8,128)S(1)}, f32[512,512]{1,0:T(8,128)S(1)}, u32[]{:S(2)}, u32[]{:S(2)}) collective-permute-start(f32[512,512]{1,0:T(8,128)S(1)} %bitcast.92), channel_id=1, source_target_pairs={{0,1},{1,0},{2,3},{3,2},{4,5},{5,4},{6,7},{7,6},{8,9},{9,8},{10,11... | collective-permute-start | bytes 3145736 | tf_op jit(solution)/shard_map/ppermute | solution.py:27
  203.9 1.8 fusion
  (122 shorter events, 37.1 us)
Async XLA Ops:
  20.9 15.7 %all-to-all-start.1 = ((f32[16,16,512]{2,1,0:T(8,128)}), f32[16,16,512]{2,1,0:T(8,128)S(1)}, u32[]{:S(2)}, u32[]{:S(2)}) async-start(f32[16,16,512]{2,1,0:T(8,128)} %bitcast.9), calls=%async_computation.1 | async-start | bytes 1048576 | tf_op jit(solution)/shard_map/all_to_all | solution.py:169
  36.6 37.6 %collective-permute-start.1 = (f32[2048,1024]{1,0:T(8,128)}, f32[2048,1024]{1,0:T(8,128)}, u32[]{:S(2)}, u32[]{:S(2)}) collective-permute-start(f32[2048,1024]{1,0:T(8,128)} %own.1), channel_id=1, source_target_pairs={{0,1},{1,0},{2,3},{3,2},{4,5},{5,4},{6,7},{7,6},{8,9},{9,8},{10,11... | collective-permute-start | bytes 25165832 | tf_op jit(solution)/shard_map/ppermute | solution.py:27
  38.2 14.8 %collective-permute-start.3 = (f32[8,16,512]{2,1,0:T(8,128)S(1)}, f32[8,16,512]{2,1,0:T(8,128)S(1)}, u32[]{:S(2)}, u32[]{:S(2)}) collective-permute-start(f32[8,16,512]{2,1,0:T(8,128)S(1)} %get-tuple-element.25), channel_id=1, source_target_pairs={{0,32},{1,33},{2,34},{3,35},{4,36},{5,37},{6,38},{7,39},{8,40},{9,... | collective-permute-start | bytes 786440 | tf_op jit(solution)/shard_map/ppermute | solution.py:43
  38.3 14.7 %collective-permute-start.4 = (f32[8,16,512]{2,1,0:T(8,128)S(1)}, f32[8,16,512]{2,1,0:T(8,128)S(1)}, u32[]{:S(2)}, u32[]{:S(2)}) collective-permute-start(f32[8,16,512]{2,1,0:T(8,128)S(1)} %get-tuple-element.25), channel_id=1, source_target_pairs={{0,64},{1,65},{2,66},{3,67},{4,68},{5,69},{6,70},{7,71},{8,72},{9,... | collective-permute-start | bytes 786440 | tf_op jit(solution)/shard_map/ppermute | solution.py:43
  40.0 13.3 %collective-permute-start.5 = (f32[8,16,512]{2,1,0:T(8,128)S(1)}, f32[8,16,512]{2,1,0:T(8,128)S(1)}, u32[]{:S(2)}, u32[]{:S(2)}) collective-permute-start(f32[8,16,512]{2,1,0:T(8,128)S(1)} %get-tuple-element.25), channel_id=1, source_target_pairs={{0,96},{1,97},{2,98},{3,99},{4,100},{5,101},{6,102},{7,103},{8,104... | collective-permute-start | bytes 786440 | tf_op jit(solution)/shard_map/ppermute | solution.py:43
  41.2 8.5 %collective-permute-start.2 = (f32[8,16,512]{2,1,0:T(8,128)S(1)}, f32[8,16,512]{2,1,0:T(8,128)S(1)}, u32[]{:S(2)}, u32[]{:S(2)}) collective-permute-start(f32[8,16,512]{2,1,0:T(8,128)S(1)} %get-tuple-element.60), channel_id=1, source_target_pairs={{0,16},{1,17},{2,18},{3,19},{4,20},{5,21},{6,22},{7,23},{8,24},{9,... | collective-permute-start | bytes 786440 | tf_op jit(solution)/shard_map/ppermute | solution.py:35
  53.5 17.9 %collective-permute-start.9 = (f32[4,8,16,256]{3,2,1,0:T(8,128)S(1)}, f32[4,8,16,256]{3,2,1,0:T(8,128)S(1)}, u32[]{:S(2)}, u32[]{:S(2)}) collective-permute-start(f32[4,8,16,256]{3,2,1,0:T(8,128)S(1)} %get-tuple-element.51.g_own), channel_id=1, source_target_pairs={{0,16},{1,17},{2,18},{3,19},{4,20},{5,21},{6,22},{7,23},{8,24},{9,... | collective-permute-start | bytes 1572872 | tf_op jit(solution)/shard_map/ppermute | solution.py:35
  55.6 14.1 %collective-permute-start.7 = (f32[2,8,16,256]{3,2,1,0:T(8,128)S(1)}, f32[2,8,16,256]{3,2,1,0:T(8,128)S(1)}, u32[]{:S(2)}, u32[]{:S(2)}) collective-permute-start(f32[2,8,16,256]{3,2,1,0:T(8,128)S(1)} %get-tuple-element.57.f0), channel_id=1, source_target_pairs={{0,64},{1,65},{2,66},{3,67},{4,68},{5,69},{6,70},{7,71},{8,72},{9,... | collective-permute-start | bytes 786440 | tf_op jit(solution)/shard_map/ppermute | solution.py:43
  58.7 11.7 %collective-permute-start.8 = (f32[2,8,16,256]{3,2,1,0:T(8,128)S(1)}, f32[2,8,16,256]{3,2,1,0:T(8,128)S(1)}, u32[]{:S(2)}, u32[]{:S(2)}) collective-permute-start(f32[2,8,16,256]{3,2,1,0:T(8,128)S(1)} %get-tuple-element.57.f0), channel_id=1, source_target_pairs={{0,96},{1,97},{2,98},{3,99},{4,100},{5,101},{6,102},{7,103},{8,104... | collective-permute-start | bytes 786440 | tf_op jit(solution)/shard_map/ppermute | solution.py:43
  63.3 39.1 %collective-permute-start.30 = (f32[128,512]{1,0:T(8,128)S(1)}, f32[128,512]{1,0:T(8,128)S(1)}, u32[]{:S(2)}, u32[]{:S(2)}) collective-permute-start(f32[128,512]{1,0:T(8,128)S(1)} %get-tuple-element.53), channel_id=1, source_target_pairs={{0,2},{1,3},{2,4},{3,5},{4,6},{5,7},{6,0},{7,1},{8,10},{9,11},{10,... | collective-permute-start | bytes 786440 | tf_op jit(solution)/shard_map/ppermute | solution.py:31
  70.5 18.2 %collective-permute-start.13 = (f32[2,8,16,256]{3,2,1,0:T(8,128)S(1)}, f32[2,8,16,256]{3,2,1,0:T(8,128)S(1)}, u32[]{:S(2)}, u32[]{:S(2)}) collective-permute-start(f32[2,8,16,256]{3,2,1,0:T(8,128)S(1)} %get-tuple-element.56.f0), channel_id=1, source_target_pairs={{0,32},{1,33},{2,34},{3,35},{4,36},{5,37},{6,38},{7,39},{8,40},{9,... | collective-permute-start | bytes 786440 | tf_op jit(solution)/shard_map/ppermute | solution.py:43
  71.2 17.6 %collective-permute-start.14 = (f32[2,8,16,256]{3,2,1,0:T(8,128)S(1)}, f32[2,8,16,256]{3,2,1,0:T(8,128)S(1)}, u32[]{:S(2)}, u32[]{:S(2)}) collective-permute-start(f32[2,8,16,256]{3,2,1,0:T(8,128)S(1)} %get-tuple-element.56.f0), channel_id=1, source_target_pairs={{0,64},{1,65},{2,66},{3,67},{4,68},{5,69},{6,70},{7,71},{8,72},{9,... | collective-permute-start | bytes 786440 | tf_op jit(solution)/shard_map/ppermute | solution.py:43
  71.4 18.4 %collective-permute-start.15 = (f32[2,8,16,256]{3,2,1,0:T(8,128)S(1)}, f32[2,8,16,256]{3,2,1,0:T(8,128)S(1)}, u32[]{:S(2)}, u32[]{:S(2)}) collective-permute-start(f32[2,8,16,256]{3,2,1,0:T(8,128)S(1)} %get-tuple-element.56.f0), channel_id=1, source_target_pairs={{0,96},{1,97},{2,98},{3,99},{4,100},{5,101},{6,102},{7,103},{8,104... | collective-permute-start | bytes 786440 | tf_op jit(solution)/shard_map/ppermute | solution.py:43
  74.2 16.1 %collective-permute-start.16 = (f32[4,8,16,256]{3,2,1,0:T(8,128)S(1)}, f32[4,8,16,256]{3,2,1,0:T(8,128)S(1)}, u32[]{:S(2)}, u32[]{:S(2)}) collective-permute-start(f32[4,8,16,256]{3,2,1,0:T(8,128)S(1)} %get-tuple-element.50.g_own), channel_id=1, source_target_pairs={{0,16},{1,17},{2,18},{3,19},{4,20},{5,21},{6,22},{7,23},{8,24},{9,... | collective-permute-start | bytes 1572872 | tf_op jit(solution)/shard_map/ppermute | solution.py:35
  88.7 15.9 %collective-permute-start.12 = (f32[2,128,256]{2,1,0:T(8,128)S(1)}, f32[2,128,256]{2,1,0:T(8,128)S(1)}, u32[]{:S(2)}, u32[]{:S(2)}) collective-permute-start(f32[2,128,256]{2,1,0:T(8,128)S(1)} %get-tuple-element.32), channel_id=1, source_target_pairs={{0,4},{1,5},{2,6},{3,7},{4,0},{5,1},{6,2},{7,3},{8,12},{9,13},{10,... | collective-permute-start | bytes 786440 | tf_op jit(solution)/shard_map/ppermute | solution.py:31
  88.8 17.0 %collective-permute-start.11 = (f32[2,128,256]{2,1,0:T(8,128)S(1)}, f32[2,128,256]{2,1,0:T(8,128)S(1)}, u32[]{:S(2)}, u32[]{:S(2)}) collective-permute-start(f32[2,128,256]{2,1,0:T(8,128)S(1)} %get-tuple-element.31), channel_id=1, source_target_pairs={{0,6},{1,7},{2,0},{3,1},{4,2},{5,3},{6,4},{7,5},{8,14},{9,15},{10,... | collective-permute-start | bytes 786440 | tf_op jit(solution)/shard_map/ppermute | solution.py:31
  89.8 16.9 %collective-permute-start.10 = (f32[2,128,256]{2,1,0:T(8,128)}, f32[2,128,256]{2,1,0:T(8,128)}, u32[]{:S(2)}, u32[]{:S(2)}) collective-permute-start(f32[2,128,256]{2,1,0:T(8,128)} %get-tuple-element.30), channel_id=1, source_target_pairs={{0,2},{1,3},{2,4},{3,5},{4,6},{5,7},{6,0},{7,1},{8,10},{9,11},{10,... | collective-permute-start | bytes 786440 | tf_op jit(solution)/shard_map/ppermute | solution.py:31
  100.2 9.9 %collective-permute-start.19 = (f32[2,128,256]{2,1,0:T(8,128)}, f32[2,128,256]{2,1,0:T(8,128)S(1)}, u32[]{:S(2)}, u32[]{:S(2)}) collective-permute-start(f32[2,128,256]{2,1,0:T(8,128)} %get-tuple-element.36), channel_id=1, source_target_pairs={{0,4},{1,5},{2,6},{3,7},{4,0},{5,1},{6,2},{7,3},{8,12},{9,13},{10,... | collective-permute-start | bytes 786440 | tf_op jit(solution)/shard_map/ppermute | solution.py:31
  102.4 23.4 %collective-permute-start.22 = (f32[4,128,256]{2,1,0:T(8,128)S(1)}, f32[4,128,256]{2,1,0:T(8,128)}, u32[]{:S(2)}, u32[]{:S(2)}) collective-permute-start(f32[4,128,256]{2,1,0:T(8,128)S(1)} %get-tuple-element.40), channel_id=1, source_target_pairs={{0,8},{1,9},{2,10},{3,11},{4,12},{5,13},{6,14},{7,15},{8,0},{9,1},... | collective-permute-start | bytes 1572872 | tf_op jit(solution)/shard_map/ppermute | solution.py:39
  104.5 10.0 %collective-permute-start.18 = (f32[2,128,256]{2,1,0:T(8,128)}, f32[2,128,256]{2,1,0:T(8,128)}, u32[]{:S(2)}, u32[]{:S(2)}) collective-permute-start(f32[2,128,256]{2,1,0:T(8,128)} %get-tuple-element.35), channel_id=1, source_target_pairs={{0,6},{1,7},{2,0},{3,1},{4,2},{5,3},{6,4},{7,5},{8,14},{9,15},{10,... | collective-permute-start | bytes 786440 | tf_op jit(solution)/shard_map/ppermute | solution.py:31
  106.5 11.6 %collective-permute-start.17 = (f32[2,128,256]{2,1,0:T(8,128)}, f32[2,128,256]{2,1,0:T(8,128)}, u32[]{:S(2)}, u32[]{:S(2)}) collective-permute-start(f32[2,128,256]{2,1,0:T(8,128)} %get-tuple-element.34), channel_id=1, source_target_pairs={{0,2},{1,3},{2,4},{3,5},{4,6},{5,7},{6,0},{7,1},{8,10},{9,11},{10,... | collective-permute-start | bytes 786440 | tf_op jit(solution)/shard_map/ppermute | solution.py:31
  106.7 14.5 %collective-permute-start.29 = (f32[128,512]{1,0:T(8,128)}, f32[128,512]{1,0:T(8,128)S(1)}, u32[]{:S(2)}, u32[]{:S(2)}) collective-permute-start(f32[128,512]{1,0:T(8,128)} %copy-done.9), channel_id=1, source_target_pairs={{0,4},{1,5},{2,6},{3,7},{4,0},{5,1},{6,2},{7,3},{8,12},{9,13},{10,... | collective-permute-start | bytes 786440 | tf_op jit(solution)/shard_map/ppermute | solution.py:31
  110.1 15.7 %collective-permute-start.28 = (f32[128,512]{1,0:T(8,128)}, f32[128,512]{1,0:T(8,128)S(1)}, u32[]{:S(2)}, u32[]{:S(2)}) collective-permute-start(f32[128,512]{1,0:T(8,128)} %copy-done.9), channel_id=1, source_target_pairs={{0,6},{1,7},{2,0},{3,1},{4,2},{5,3},{6,4},{7,5},{8,14},{9,15},{10,... | collective-permute-start | bytes 786440 | tf_op jit(solution)/shard_map/ppermute | solution.py:31
  114.6 12.9 %collective-permute-start.27 = (f32[128,512]{1,0:T(8,128)}, f32[128,512]{1,0:T(8,128)S(1)}, u32[]{:S(2)}, u32[]{:S(2)}) collective-permute-start(f32[128,512]{1,0:T(8,128)} %get-tuple-element.52), channel_id=1, source_target_pairs={{0,8},{1,9},{2,10},{3,11},{4,12},{5,13},{6,14},{7,15},{8,0},{9,1},... | collective-permute-start | bytes 786440 | tf_op jit(solution)/shard_map/ppermute | solution.py:39
  118.1 17.4 %collective-permute-start.21 = (f32[4,128,256]{2,1,0:T(8,128)S(1)}, f32[4,128,256]{2,1,0:T(8,128)S(1)}, u32[]{:S(2)}, u32[]{:S(2)}) collective-permute-start(f32[4,128,256]{2,1,0:T(8,128)S(1)} %get-tuple-element.38), channel_id=1, source_target_pairs={{0,8},{1,9},{2,10},{3,11},{4,12},{5,13},{6,14},{7,15},{8,0},{9,1},... | collective-permute-start | bytes 1572872 | tf_op jit(solution)/shard_map/ppermute | solution.py:39
  138.1 29.8 %all-to-all-start.2 = ((f32[64,8,512]{2,1,0:T(8,128)}), f32[64,8,512]{2,1,0:T(8,128)S(1)}, u32[]{:S(2)}, u32[]{:S(2)}) async-start(f32[64,8,512]{2,1,0:T(8,128)} %bitcast.42), calls=%async_computation.2 | async-start | bytes 2097152 | tf_op jit(solution)/shard_map/all_to_all | solution.py:222
  169.1 22.2 %all-to-all-start.3 = ((f32[64,8,512]{2,1,0:T(8,128)}), f32[64,8,512]{2,1,0:T(8,128)S(1)}, u32[]{:S(2)}, u32[]{:S(2)}) async-start(f32[64,8,512]{2,1,0:T(8,128)} %broadcast_in_dim.9), calls=%async_computation.3 | async-start | bytes 2097152 | tf_op jit(solution)/shard_map/all_to_all | solution.py:225
  174.9 23.6 %collective-permute-start.20 = (f32[2,128,256]{2,1,0:T(8,128)}, f32[2,128,256]{2,1,0:T(8,128)S(1)}, u32[]{:S(2)}, u32[]{:S(2)}) collective-permute-start(f32[2,128,256]{2,1,0:T(8,128)} %fusion.5), channel_id=1, source_target_pairs={{0,8},{1,9},{2,10},{3,11},{4,12},{5,13},{6,14},{7,15},{8,0},{9,1},... | collective-permute-start | bytes 786440 | tf_op jit(solution)/shard_map/ppermute | solution.py:39
  179.2 19.4 %collective-permute-start.25 = (f32[2,128,256]{2,1,0:T(8,128)}, f32[2,128,256]{2,1,0:T(8,128)S(1)}, u32[]{:S(2)}, u32[]{:S(2)}) collective-permute-start(f32[2,128,256]{2,1,0:T(8,128)} %get-tuple-element.48), channel_id=1, source_target_pairs={{0,4},{1,5},{2,6},{3,7},{4,0},{5,1},{6,2},{7,3},{8,12},{9,13},{10,... | collective-permute-start | bytes 786440 | tf_op jit(solution)/shard_map/ppermute | solution.py:31
  181.8 16.7 %collective-permute-start.24 = (f32[2,128,256]{2,1,0:T(8,128)}, f32[2,128,256]{2,1,0:T(8,128)S(1)}, u32[]{:S(2)}, u32[]{:S(2)}) collective-permute-start(f32[2,128,256]{2,1,0:T(8,128)} %get-tuple-element.49), channel_id=1, source_target_pairs={{0,6},{1,7},{2,0},{3,1},{4,2},{5,3},{6,4},{7,5},{8,14},{9,15},{10,... | collective-permute-start | bytes 786440 | tf_op jit(solution)/shard_map/ppermute | solution.py:31
  182.7 17.2 %collective-permute-start.23 = (f32[2,128,256]{2,1,0:T(8,128)}, f32[2,128,256]{2,1,0:T(8,128)}, u32[]{:S(2)}, u32[]{:S(2)}) collective-permute-start(f32[2,128,256]{2,1,0:T(8,128)} %get-tuple-element.47), channel_id=1, source_target_pairs={{0,2},{1,3},{2,4},{3,5},{4,6},{5,7},{6,0},{7,1},{8,10},{9,11},{10,... | collective-permute-start | bytes 786440 | tf_op jit(solution)/shard_map/ppermute | solution.py:31
  191.3 12.6 %collective-permute-start.31 = (f32[512,512]{1,0:T(8,128)S(1)}, f32[512,512]{1,0:T(8,128)S(1)}, u32[]{:S(2)}, u32[]{:S(2)}) collective-permute-start(f32[512,512]{1,0:T(8,128)S(1)} %bitcast.92), channel_id=1, source_target_pairs={{0,1},{1,0},{2,3},{3,2},{4,5},{5,4},{6,7},{7,6},{8,9},{9,8},{10,11... | collective-permute-start | bytes 3145736 | tf_op jit(solution)/shard_map/ppermute | solution.py:27
  (26 other events, 284.3 us)
where the time goes:
time: 207 us; the launch traced here: 206 us
  waiting for transfers between devices  73.7 us (36%)
  starting transfers between devices  65.2 us (31%)
  Pallas kernels  19.6 us (9%)
  blocking collectives  19.1 us (9%)
  other arithmetic  12.7 us (6%)
  local copies, waits for them, and re-layouts  11.3 us (5%)
  matrix products  3.16 us (2%)
    pallas_call x2, Pallas kernels, panel(): pl.pallas_call(panel_kernel, grid_spec=pltpu.PrefetchScalarGridSpec(num_s...  19.6 us
    all_to_all x1, blocking collectives, per_device(): spread = lax.all_to_all(factor.reshape(2, 8, 16, WIDTH), ROW, 1, 0)  19.1 us
    all_to_all x1, waiting for transfers between devices, per_device(): diag = lax.all_to_all(diag.reshape(64, 8, WIDTH), CHIPS, 0, 0)  18.2 us
    ppermute x9, waiting for transfers between devices, to_z(): return lax.ppermute(v, AXES, route(lambda z, y, x, c: (z + s, y, x, c)))  12 us
    ppermute x12, starting transfers between devices, to_x(): return lax.ppermute(v, AXES, route(lambda z, y, x, c: (z, y, x + s, c)))  11.7 us
    all_to_all x1, starting transfers between devices, per_device(): diag = lax.all_to_all(diag.reshape(64, 8, WIDTH), CHIPS, 0, 0)  11.7 us
    ppermute x12, waiting for transfers between devices, to_x(): return lax.ppermute(v, AXES, route(lambda z, y, x, c: (z, y, x + s, c)))  10.3 us
    ppermute x9, starting transfers between devices, to_z(): return lax.ppermute(v, AXES, route(lambda z, y, x, c: (z + s, y, x, c)))  9.82 us
  transfers between devices with their start and end apart: 35, of which 15 were waited for; matrix products, arithmetic and copies ran while one was open for 6% of the time, Pallas kernels for 10%

commit v1 on v0

v1 whole, which is shorter than its diff:
```python
import jax
import jax.numpy as jnp
from jax import lax
from jax.experimental import pallas as pl
from jax.experimental.pallas import tpu as pltpu
from jax.sharding import Mesh
from jax.sharding import PartitionSpec as P

TILE = 512
WIDTH = 512

ROW, COL = ("z", "yh"), ("yl", "x", "core")
AXES, CHIPS = ROW + COL, ROW + COL[:2]


def route(move):
    pairs = []
    for d in range(128):
        z, yh, yl, x, core = d // 32, d // 16 % 2, d // 8 % 2, d // 2 % 4, d % 2
        z, y, x, core = move(z, yh * 2 + yl, x, core)
        z, y, x = z % 4, y % 4, x % 4
        pairs.append((d, z * 32 + (y // 2) * 16 + (y % 2) * 8 + x * 2 + core))
    return pairs


def to_core(v):
    return lax.ppermute(v, AXES, route(lambda z, y, x, c: (z, y, x, 1 - c)))


def to_x(v, s):
    return lax.ppermute(v, AXES, route(lambda z, y, x, c: (z, y, x + s, c)))


def to_y(v, s):
    return lax.ppermute(v, AXES, route(lambda z, y, x, c: (z, y + s, x, c)))


def to_yl(v):
    return lax.ppermute(v, AXES, route(lambda z, y, x, c: (z, y ^ 1, x, c)))


def to_z(v, s):
    return lax.ppermute(v, AXES, route(lambda z, y, x, c: (z + s, y, x, c)))


def halves(a):
    hi = a.astype(jnp.bfloat16)
    return hi, (a - hi.astype(jnp.float32)).astype(jnp.bfloat16)


def prepare_kernel(a, hi, lo):
    def step(a, hi, lo):
        hi[...], lo[...] = halves(a[...])

    spec = pl.BlockSpec((256, a.shape[1]), lambda i: (i, 0))
    pltpu.emit_pipeline(
        step, grid=(a.shape[0] // 256,), in_specs=[spec], out_specs=[spec, spec]
    )(a, hi, lo)


def prepare(a):
    spec = pl.BlockSpec(memory_space=pltpu.HBM)
    out = jax.ShapeDtypeStruct(a.shape, jnp.bfloat16)
    return pl.pallas_call(
        prepare_kernel,
        in_specs=[spec],
        out_specs=[spec, spec],
        out_shape=[out, out],
        compiler_params=pltpu.CompilerParams(vmem_limit_bytes=54 << 20),
        cost_estimate=pl.CostEstimate(
            flops=4 * a.size, bytes_accessed=8 * a.size, transcendentals=0
        ),
    )(a)


def panel_kernel(info, own_hi, own_lo, oth_hi, oth_lo, *rest):
    (f0, f1, f2, f3, g_own, g_oth), outs, (f_hi, f_lo, acc) = rest[:6], rest[6:12], rest[12:]
    core, z, yh, x, yl = info[8], info[9], info[10], info[11], info[12]

    def place(value, col, row):
        at = pl.ds(pl.multiple_of(col * 128 + row * 16, 16), 16)
        hi, lo = halves(value)
        f_hi[at, :] = hi
        f_lo[at, :] = lo

    i = pl.program_id(0)

    @pl.when(i == 0)
    def _():
        for s, ref in enumerate((f0, f1, f2, f3)):
            from_z = lax.rem(z + 4 - s, 4)
            for h, from_yh in enumerate((yh, 1 - yh)):
                for col in range(8):
                    place(ref[h, col], col, from_z * 2 + from_yh)

        for ref, from_yh in ((g_own, yh), (g_oth, 1 - yh)):
            for s in range(4):
                from_z = lax.rem(z + 4 - s, 4)
                for col in range(8):
                    place(ref[s, col], col + 8, from_z * 2 + from_yh)

    acc[...] = jnp.zeros_like(acc)
    for a_hi, a_lo, side in ((own_hi, own_lo, core), (oth_hi, oth_lo, 1 - core)):
        for j in range(2):
            tile = side * 2 + j

            @pl.when((info[i] > 0) & (info[4 + tile] > 0))
            def _():
                at = pl.ds(pl.multiple_of(tile * TILE, TILE), TILE)
                cols = slice(j * TILE, (j + 1) * TILE)
                hi, b_hi = a_hi[:, cols], f_hi[at, :]
                acc[...] += (
                    jnp.dot(hi, b_hi, preferred_element_type=jnp.float32)
                    + jnp.dot(a_lo[:, cols], b_hi, preferred_element_type=jnp.float32)
                    + jnp.dot(hi, f_lo[at, :], preferred_element_type=jnp.float32)
                )

    to_l = lax.div(i, 2)
    for b in range(2):
        step = lax.rem(lax.rem(i, 2) * 2 + b + 4 - x, 4)
        first = acc[b * 256 : b * 256 + 128, :]
        last = acc[b * 256 + 128 : b * 256 + 256, :]
        for s in range(4):

            @pl.when(step == s)
            def _():
                outs[s][to_l] = first

        @pl.when(to_l == yl)
        def _():
            outs[4][step] = last

        @pl.when(to_l != yl)
        def _():
            outs[5][step] = last


def in_vmem(n):
    return [pl.BlockSpec(memory_space=pltpu.VMEM)] * n


def panel(info, sides, pieces):
    cols = pieces[0].shape[-1]
    whole = lambda v: pl.BlockSpec(v.shape, lambda i, info: (0,) * len(v.shape))
    block = pl.BlockSpec((TILE, sides[0].shape[1]), lambda i, info: (info[13 + i], 0))
    out = [jax.ShapeDtypeStruct((2, 128, cols), jnp.float32)] * 4
    out += [jax.ShapeDtypeStruct((4, 128, cols), jnp.float32)] * 2
    return pl.pallas_call(
        panel_kernel,
        grid_spec=pltpu.PrefetchScalarGridSpec(
            num_scalar_prefetch=1,
            grid=(4,),
            in_specs=[block] * 4 + [whole(v) for v in pieces],
            out_specs=[whole(v) for v in out],
            scratch_shapes=[
                pltpu.VMEM((2048, cols), jnp.bfloat16),
                pltpu.VMEM((2048, cols), jnp.bfloat16),
                pltpu.VMEM((TILE, cols), jnp.float32),
            ],
        ),
        out_shape=out,
        compiler_params=pltpu.CompilerParams(vmem_limit_bytes=48 << 20),
        cost_estimate=pl.CostEstimate(
            flops=3 * 2 * 2048 * 2048 * cols,
            bytes_accessed=20 << 20,
            transcendentals=0,
        ),
    )(info, *sides, *pieces)


def finish_kernel(info, *refs):
    parts, rows, (diag, keep, send, *lasts) = refs[:12], refs[12:18], refs[18:]
    yl = info[12]
    t_hi, t_lo = halves(jnp.concatenate([ref[...] for ref in rows], axis=1))
    for c in range(2):
        firsts, (mine, got) = parts[c * 6 : c * 6 + 4], parts[c * 6 + 4 : c * 6 + 6]
        here, away = (sum(ref[i] for ref in firsts) for i in (yl, 1 - yl))
        sums = [here, away] + [mine[s] + got[s] for s in range(4)]
        for ref, value in zip((keep, send, *lasts), sums):
            ref[c] = value
        p_hi, p_lo = halves(jnp.concatenate(sums, axis=0))
        cols = p_hi.shape[1]
        diag[:, c * cols : (c + 1) * cols] = (
            jnp.dot(t_hi, p_hi, preferred_element_type=jnp.float32)
            + jnp.dot(t_lo, p_hi, preferred_element_type=jnp.float32)
            + jnp.dot(t_hi, p_lo, preferred_element_type=jnp.float32)
        )


def finish(info, parts, rows):
    cols = parts[0].shape[-1]
    out = [jax.ShapeDtypeStruct((WIDTH, 2 * cols), jnp.float32)]
    out += [jax.ShapeDtypeStruct((2, 128, cols), jnp.float32)] * 6
    return pl.pallas_call(
        finish_kernel,
        in_specs=[pl.BlockSpec(memory_space=pltpu.SMEM)] + in_vmem(18),
        out_specs=in_vmem(7),
        out_shape=out,
        compiler_params=pltpu.CompilerParams(vmem_limit_bytes=24 << 20),
        cost_estimate=pl.CostEstimate(
            flops=3 * 4 * 768 * WIDTH * cols, bytes_accessed=9 << 20, transcendentals=0
        ),
    )(info, *parts, *rows)


def pick(v, i):
    return lax.dynamic_index_in_dim(v, i, 0, keepdims=False)


def per_device(ancestor, factor, diag_inverse, structure):
    z, yh, yl, x, core = (lax.axis_index(axis) for axis in AXES)
    row, group = z * 2 + yh, yl * 4 + x
    at_first = core == 0
    half = WIDTH // 2

    listed = pick(structure, core)
    four = jnp.arange(4, dtype=jnp.int32)
    flag = lambda tiles: jnp.any(listed[None, :] == tiles[:, None], axis=1)
    rows_on = flag(row * 4 + four)
    past = jnp.where(rows_on[None, :] & (four[None, :] <= four[:, None]), four[None, :], 0)
    info = jnp.concatenate(
        [
            rows_on.astype(jnp.int32),
            flag(group * 4 + four).astype(jnp.int32),
            jnp.stack([core, z, yh, x, yl]).astype(jnp.int32),
            jnp.max(past, axis=1),
        ]
    )

    oth = to_core(ancestor)
    sides = prepare(ancestor)
    sides = [*sides, *prepare(oth)]

    turned = jnp.swapaxes(factor, 1, 2)
    f_keep = pick(turned, core)
    f_got = to_core(pick(turned, 1 - core))
    f_first = jnp.where(at_first, f_keep, f_got)
    f_last = jnp.where(at_first, f_got, f_keep)
    f_rows = [f_first, to_yl(f_first), f_last, *(to_x(f_last, s) for s in (3, 2, 1))]

    spread = lax.all_to_all(factor.reshape(2, 8, 16, WIDTH), ROW, 1, 0)
    spread = lax.all_to_all(spread.reshape(16, 16, WIDTH), COL, 0, 0)
    low, high = spread[:8], spread[8:]
    low_y, *high_z = lax.optimization_barrier(
        (to_y(low, 2), high, *(to_z(high, s) for s in (1, 2, 3)))
    )
    pair = jnp.stack([low, low_y])
    quad = jnp.stack(high_z)

    gathered = []
    for c in range(2):
        cut = lambda v: v[..., c * half : (c + 1) * half]
        pairs = [cut(pair)] + [to_z(cut(pair), s) for s in (1, 2, 3)]
        gathered.append([*pairs, cut(quad), to_y(cut(quad), 2)])

    parts = []
    for c in range(2):
        first0, first1, first2, first3, last_keep, last_send = panel(
            info, sides, gathered[c]
        )
        got = [to_x(first1, 1), to_x(first3, 3), to_x(first2, 2)]
        parts += [first0, *got, last_keep, to_yl(last_send)]

    diag, first, first_send, *last = finish(info, parts, f_rows)
    first = first + to_yl(first_send)
    last = last[0] + to_x(last[1], 1) + to_x(last[3], 3) + to_x(last[2], 2)
    mine = jnp.where(at_first, first, last)
    theirs = to_core(jnp.where(at_first, last, first))
    off = -jnp.where(at_first, jnp.stack([mine, theirs]), jnp.stack([theirs, mine]))
    off = jnp.concatenate([off[:, 0], off[:, 1]], axis=-1)

    diag = lax.all_to_all(diag.reshape(64, 8, WIDTH), CHIPS, 0, 0)
    own8 = ((row * 2 + yl) * 4 + x) * 8
    diag = jnp.sum(diag, axis=0)
    diag = diag + lax.dynamic_slice(diag_inverse, (core, own8, 0), (1, 8, WIDTH))[0]
    diag = lax.all_to_all(jnp.broadcast_to(diag, (64, 8, WIDTH)), CHIPS, 0, 0)
    diag = diag.reshape(WIDTH, WIDTH)
    diag_oth = to_core(diag)
    both = jnp.where(
        at_first, jnp.stack([diag, diag_oth]), jnp.stack([diag_oth, diag])
    )
    return off, both


def solution(mesh):
    mesh = Mesh(mesh.devices.reshape(4, 2, 2, 4, 2), AXES)
    in_specs = (P(ROW, COL), P(None, AXES, None), P(), P())
    out_specs = (P(None, AXES, None), P())

    return jax.shard_map(
        per_device, mesh=mesh, in_specs=in_specs, out_specs=out_specs, check_vma=False
    )
```

time: 207 us -> 202 us (0.976)
  Pallas kernels: 19.6 us -> 38.1 us
  waiting for transfers between devices: 73.7 us -> 65.3 us
  other arithmetic: 12.7 us -> 4.95 us
  local copies, waits for them, and re-layouts: 11.3 us -> 3.61 us
  starting transfers between devices: 65.2 us -> 69.4 us
  matrix products: 3.16 us -> 0 us
    pallas_call x0 -> x3, Pallas kernels: none -> 21.7 us  [the longest x2 18.6 us: prepare(): pl.pallas_call(prepare_kernel, in_specs=[spec], out_specs=[spec, spec], o...]
    ppermute x12, waiting for transfers between devices: 10.3 us -> 18.2 us  [to_x(): return lax.ppermute(v, AXES, route(lambda z, y, x, c: (z, y, x + s, c)))]
    ppermute x9, waiting for transfers between devices: 12 us -> 4.39 us  [to_z(): return lax.ppermute(v, AXES, route(lambda z, y, x, c: (z + s, y, x, c)))]
    ppermute x4, starting transfers between devices: 9.35 us -> 16.9 us  [to_core(): return lax.ppermute(v, AXES, route(lambda z, y, x, c: (z, y, x, 1 - c)))]
    ppermute x3, waiting for transfers between devices: 7.25 us -> 0.01 us  [to_y(): return lax.ppermute(v, AXES, route(lambda z, y, x, c: (z, y + s, x, c)))]
    unnamed x46 -> x12, local copies, waits for them, and re-layouts: 7.3 us -> 0.97 us
    ppermute x4, waiting for transfers between devices: 7.55 us -> 3.41 us  [to_yl(): return lax.ppermute(v, AXES, route(lambda z, y, x, c: (z, y ^ 1, x, c)))]
    add x3 -> x1, other arithmetic: 4.19 us -> 0.73 us  [per_device(): diag + lax.dynamic_slice(diag_inverse, (core, own8, 0), (1, 8, WIDTH))[0]]
  transfers between devices with their start and end apart: 35 -> 35, of which waited for: 15 -> 11; matrix products, arithmetic and copies ran while one was open for 6% -> 2% of each run, Pallas kernels for 10% -> 17%
where the time goes in v1:
time: 202 us; the launch traced here: 201 us
  starting transfers between devices  69.4 us (34%)
  waiting for transfers between devices  65.3 us (32%)
  Pallas kernels  38.1 us (19%)
  blocking collectives  19.1 us (9%)
  other arithmetic  4.95 us (2%)
  local copies, waits for them, and re-layouts  3.61 us (2%)
    all_to_all x1, blocking collectives, per_device(): spread = lax.all_to_all(factor.reshape(2, 8, 16, WIDTH), ROW, 1, 0)  19.1 us
    pallas_call x2, Pallas kernels, prepare(): pl.pallas_call(prepare_kernel, in_specs=[spec], out_specs=[spec, spec], o...  18.6 us
    ppermute x12, waiting for transfers between devices, to_x(): return lax.ppermute(v, AXES, route(lambda z, y, x, c: (z, y, x + s, c)))  18.2 us
    all_to_all x1, waiting for transfers between devices, per_device(): diag = lax.all_to_all(diag.reshape(64, 8, WIDTH), CHIPS, 0, 0)  17.3 us
    ppermute x4, starting transfers between devices, to_core(): return lax.ppermute(v, AXES, route(lambda z, y, x, c: (z, y, x, 1 - c)))  16.9 us
    pallas_call x2, Pallas kernels, panel(): pl.pallas_call(panel_kernel, grid_spec=pltpu.PrefetchScalarGridSpec(num_s...  16.5 us
    ppermute x12, starting transfers between devices, to_x(): return lax.ppermute(v, AXES, route(lambda z, y, x, c: (z, y, x + s, c)))  13.6 us
    all_to_all x1, waiting for transfers between devices, per_device(): diag = lax.all_to_all(jnp.broadcast_to(diag, (64, 8, WIDTH)), CHIPS, 0, 0)  11.3 us
  transfers between devices with their start and end apart: 35, of which 11 were waited for; matrix products, arithmetic and copies ran while one was open for 2% of the time, Pallas kernels for 17%

profile of v1, /device:TPU:1, one launch (start us, length us, event | category | flops | bytes accessed | tf_op | source)
XLA Modules:
  0.0 201.4 jit_solution(7777182140744739623)
XLA Ops:
  3.3 19.1 %all_to_all.30 = f32[1,2,8,16,512]{4,3,1,0,2:T(8,128)} all-to-all(f32[1,2,8,16,512]{4,3,1,0,2:T(8,128)S(1)} %copy.17), channel_id=1, replica_groups=mesh['z'=4,'yh'=2,'yl'=2,'x'=4,'core'=2] {'z','yh'}, dimensions={2} | all-to-all | bytes 1048576 | tf_op jit(solution)/shard_map/all_to_all | solution.py:241
  22.3 5.6 %all-to-all-start.1 = ((f32[16,16,512]{2,1,0:T(8,128)}), f32[16,16,512]{2,1,0:T(8,128)S(1)}, u32[]{:S(2)}, u32[]{:S(2)}) async-start(f32[16,16,512]{2,1,0:T(8,128)} %bitcast.9), calls=%async_computation.1 | async-start | bytes 1048576 | tf_op jit(solution)/shard_map/all_to_all | solution.py:242
  27.9 9.5 %all-to-all-done.1 = f32[16,16,512]{2,1,0:T(8,128)S(1)} async-done(((f32[16,16,512]{2,1,0:T(8,128)}), f32[16,16,512]{2,1,0:T(8,128)S(1)}, u32[]{:S(2)}, u32[]{:S(2)}) %all-to-all-start.1) | async-done | bytes 524320 | tf_op jit(solution)/shard_map/all_to_all | solution.py:242
  37.6 1.7 collective-permute-start.3
  41.7 4.4 %collective-permute-done.2 = f32[8,16,512]{2,1,0:T(8,128)S(1)} collective-permute-done((f32[8,16,512]{2,1,0:T(8,128)S(1)}, f32[8,16,512]{2,1,0:T(8,128)S(1)}, u32[]{:S(2)}, u32[]{:S(2)}) %collective-permute-start.2) | collective-permute-done | bytes 262176 | tf_op jit(solution)/shard_map/ppermute | solution.py:43
  46.1 7.0 %collective-permute-start.21 = (f32[512,128]{1,0:T(8,128)S(1)}, f32[512,128]{1,0:T(8,128)S(1)}, u32[]{:S(2)}, u32[]{:S(2)}) collective-permute-start(f32[512,128]{1,0:T(8,128)S(1)} %bitcast.48), channel_id=1, source_target_pairs={{0,1},{1,0},{2,3},{3,2},{4,5},{5,4},{6,7},{7,6},{8,9},{9,8},{10,11... | collective-permute-start | bytes 786440 | tf_op jit(solution)/shard_map/ppermute | solution.py:27
  55.1 3.1 %collective-permute-start.14 = (f32[2,8,16,256]{3,2,1,0:T(8,128)S(1)}, f32[2,8,16,256]{3,2,1,0:T(8,128)S(1)}, u32[]{:S(2)}, u32[]{:S(2)}) collective-permute-start(f32[2,8,16,256]{3,2,1,0:T(8,128)S(1)} %get-tuple-element.70.rest_0_), channel_id=1, source_target_pairs={{0,64},{1,65},{2,66},{3,67},{4,68},{5,69},{6,70},{7,71},{8,72},{9,... | collective-permute-start | bytes 786440 | tf_op jit(solution)/shard_map/ppermute | solution.py:43
  59.3 9.3 %shard_map.59 = (bf16[2048,1024]{1,0:T(8,128)(2,1)}, bf16[2048,1024]{1,0:T(8,128)(2,1)}) custom-call(f32[2048,1024]{1,0:T(8,128)} %a.1), custom_call_target="tpu_custom_call" | custom-call | flops 8388608 | bytes 16777216 | tf_op jit(solution)/shard_map/pallas_call | solution.py:64
  68.7 1.6 collective-permute-start.23
  70.3 9.3 %shard_map.60 = (bf16[2048,1024]{1,0:T(8,128)(2,1)}, bf16[2048,1024]{1,0:T(8,128)(2,1)}) custom-call(f32[2048,1024]{1,0:T(8,128)} %collective-permute-done.a), custom_call_target="tpu_custom_call" | custom-call | flops 8388608 | bytes 16777216 | tf_op jit(solution)/shard_map/pallas_call | solution.py:64
  81.5 2.1 %collective-permute-start.7 = (f32[2,8,16,256]{3,2,1,0:T(8,128)S(1)}, f32[2,8,16,256]{3,2,1,0:T(8,128)S(1)}, u32[]{:S(2)}, u32[]{:S(2)}) collective-permute-start(f32[2,8,16,256]{3,2,1,0:T(8,128)S(1)} %get-tuple-element.71.rest_0_), channel_id=1, source_target_pairs={{0,96},{1,97},{2,98},{3,99},{4,100},{5,101},{6,102},{7,103},{8,104... | collective-permute-start | bytes 786440 | tf_op jit(solution)/shard_map/ppermute | solution.py:43
  83.6 2.1 %collective-permute-start.8 = (f32[4,8,16,256]{3,2,1,0:T(8,128)S(1)}, f32[4,8,16,256]{3,2,1,0:T(8,128)S(1)}, u32[]{:S(2)}, u32[]{:S(2)}) collective-permute-start(f32[4,8,16,256]{3,2,1,0:T(8,128)S(1)} %get-tuple-element.63.rest_4_), channel_id=1, source_target_pairs={{0,16},{1,17},{2,18},{3,19},{4,20},{5,21},{6,22},{7,23},{8,24},{9,... | collective-permute-start | bytes 1572872 | tf_op jit(solution)/shard_map/ppermute | solution.py:35
  85.7 8.2 %shard_map.62 = (f32[2,128,256]{2,1,0:T(8,128)S(1)}, f32[2,128,256]{2,1,0:T(8,128)S(1)}, f32[2,128,256]{2,1,0:T(8,128)S(1)}, f32[2,128,256]{2,1,0:T(8,128)S(1)},...) custom-call(s32[17]{0:T(128)S(1)} %concatenate.6.info, bf16[2048,1024]{1,0:T(8,128)(2,1)} %get-tuple-element.30.own_hi, ...), custom_call_target="tpu_custom_call" | custom-call | flops 6442450944 | bytes 20971520 | tf_op jit(solution)/shard_map/pallas_call | solution.py:148
  94.1 2.6 %collective-permute-start.22 = (f32[512,128]{1,0:T(8,128)S(1)}, f32[512,128]{1,0:T(8,128)S(1)}, u32[]{:S(2)}, u32[]{:S(2)}) collective-permute-start(f32[512,128]{1,0:T(8,128)S(1)} %get-tuple-element.67.refs_12_), channel_id=1, source_target_pairs={{0,8},{1,9},{2,10},{3,11},{4,12},{5,13},{6,14},{7,15},{8,0},{9,1},... | collective-permute-start | bytes 786440 | tf_op jit(solution)/shard_map/ppermute | solution.py:39
  96.9 8.2 %shard_map.61 = (f32[2,128,256]{2,1,0:T(8,128)S(1)}, f32[2,128,256]{2,1,0:T(8,128)S(1)}, f32[2,128,256]{2,1,0:T(8,128)S(1)}, f32[2,128,256]{2,1,0:T(8,128)S(1)},...) custom-call(s32[17]{0:T(128)S(1)} %concatenate.6.info, bf16[2048,1024]{1,0:T(8,128)(2,1)} %get-tuple-element.30.own_hi, ...), custom_call_target="tpu_custom_call" | custom-call | flops 6442450944 | bytes 20971520 | tf_op jit(solution)/shard_map/pallas_call | solution.py:148
  105.2 1.8 collective-permute-start.18
  107.0 2.6 %collective-permute-start.19 = (f32[2,128,256]{2,1,0:T(8,128)S(1)}, f32[2,128,256]{2,1,0:T(8,128)S(1)}, u32[]{:S(2)}, u32[]{:S(2)}) collective-permute-start(f32[2,128,256]{2,1,0:T(8,128)S(1)} %get-tuple-element.48), channel_id=1, source_target_pairs={{0,4},{1,5},{2,6},{3,7},{4,0},{5,1},{6,2},{7,3},{8,12},{9,13},{10,... | collective-permute-start | bytes 786440 | tf_op jit(solution)/shard_map/ppermute | solution.py:31
  111.1 4.5 %collective-permute-done.17.refs_7_ = f32[2,128,256]{2,1,0:T(8,128)S(1)} collective-permute-done((f32[2,128,256]{2,1,0:T(8,128)S(1)}, f32[2,128,256]{2,1,0:T(8,128)S(1)}, u32[]{:S(2)}, u32[]{:S(2)}) %collective-permute-start.17) | collective-permute-done | bytes 262176 | tf_op jit(solution)/shard_map/ppermute | solution.py:31
  116.4 2.7 %collective-permute-done.19.refs_9_ = f32[2,128,256]{2,1,0:T(8,128)S(1)} collective-permute-done((f32[2,128,256]{2,1,0:T(8,128)S(1)}, f32[2,128,256]{2,1,0:T(8,128)S(1)}, u32[]{:S(2)}, u32[]{:S(2)}) %collective-permute-start.19) | collective-permute-done | bytes 262176 | tf_op jit(solution)/shard_map/ppermute | solution.py:31
  119.1 2.1 %collective-permute-start.9 = (f32[2,128,256]{2,1,0:T(8,128)S(1)}, f32[2,128,256]{2,1,0:T(8,128)S(1)}, u32[]{:S(2)}, u32[]{:S(2)}) collective-permute-start(f32[2,128,256]{2,1,0:T(8,128)S(1)} %get-tuple-element.40), channel_id=1, source_target_pairs={{0,2},{1,3},{2,4},{3,5},{4,6},{5,7},{6,0},{7,1},{8,10},{9,11},{10,... | collective-permute-start | bytes 786440 | tf_op jit(solution)/shard_map/ppermute | solution.py:31
  121.2 4.2 %collective-permute-done.10.refs_2_ = f32[2,128,256]{2,1,0:T(8,128)S(1)} collective-permute-done((f32[2,128,256]{2,1,0:T(8,128)S(1)}, f32[2,128,256]{2,1,0:T(8,128)S(1)}, u32[]{:S(2)}, u32[]{:S(2)}) %collective-permute-start.10) | collective-permute-done | bytes 262176 | tf_op jit(solution)/shard_map/ppermute | solution.py:31
  125.4 5.2 %collective-permute-done.9.refs_1_ = f32[2,128,256]{2,1,0:T(8,128)S(1)} collective-permute-done((f32[2,128,256]{2,1,0:T(8,128)S(1)}, f32[2,128,256]{2,1,0:T(8,128)S(1)}, u32[]{:S(2)}, u32[]{:S(2)}) %collective-permute-start.9) | collective-permute-done | bytes 262176 | tf_op jit(solution)/shard_map/ppermute | solution.py:31
  130.6 3.4 %collective-permute-done.12.refs_5_ = f32[4,128,256]{2,1,0:T(8,128)S(1)} collective-permute-done((f32[4,128,256]{2,1,0:T(8,128)S(1)}, f32[4,128,256]{2,1,0:T(8,128)S(1)}, u32[]{:S(2)}, u32[]{:S(2)}) %collective-permute-start.12) | collective-permute-done | bytes 524320 | tf_op jit(solution)/shard_map/ppermute | solution.py:39
  134.0 3.0 %shard_map.63 = (f32[512,512]{1,0:T(8,128)}, f32[2,128,256]{2,1,0:T(8,128)S(1)}, f32[2,128,256]{2,1,0:T(8,128)S(1)}, f32[2,128,256]{2,1,0:T(8,128)S(1)}, f32[2,1...) custom-call(s32[17]{0:T(128)S(1)} %concatenate.6.info, ...), custom_call_target="tpu_custom_call" | custom-call | flops 1207959552 | bytes 9437184 | tf_op jit(solution)/shard_map/pallas_call | solution.py:194
  137.0 8.4 %all-to-all-start.2 = ((f32[64,8,512]{2,1,0:T(8,128)}), f32[64,8,512]{2,1,0:T(8,128)S(1)}, u32[]{:S(2)}, u32[]{:S(2)}) async-start(f32[64,8,512]{2,1,0:T(8,128)} %bitcast.25), calls=%async_computation.2 | async-start | bytes 2097152 | tf_op jit(solution)/shard_map/all_to_all | solution.py:272
  145.4 17.3 %all-to-all-done.2 = f32[64,8,512]{2,1,0:T(8,128)S(1)} async-done(((f32[64,8,512]{2,1,0:T(8,128)}), f32[64,8,512]{2,1,0:T(8,128)S(1)}, u32[]{:S(2)}, u32[]{:S(2)}) %all-to-all-start.2) | async-done | bytes 1048608 | tf_op jit(solution)/shard_map/all_to_all | solution.py:272
  164.7 5.2 %all-to-all-start.3 = ((f32[64,8,512]{2,1,0:T(8,128)}), f32[64,8,512]{2,1,0:T(8,128)S(1)}, u32[]{:S(2)}, u32[]{:S(2)}) async-start(f32[64,8,512]{2,1,0:T(8,128)} %broadcast_in_dim.9), calls=%async_computation.3 | async-start | bytes 2097152 | tf_op jit(solution)/shard_map/all_to_all | solution.py:276
  175.2 11.3 %all-to-all-done.3 = f32[64,8,512]{2,1,0:T(8,128)S(1)} async-done(((f32[64,8,512]{2,1,0:T(8,128)}), f32[64,8,512]{2,1,0:T(8,128)S(1)}, u32[]{:S(2)}, u32[]{:S(2)}) %all-to-all-start.3) | async-done | bytes 1048608 | tf_op jit(solution)/shard_map/all_to_all | solution.py:276
  186.5 5.5 %collective-permute-start.31 = (f32[512,512]{1,0:T(8,128)S(1)}, f32[512,512]{1,0:T(8,128)S(1)}, u32[]{:S(2)}, u32[]{:S(2)}) collective-permute-start(f32[512,512]{1,0:T(8,128)S(1)} %bitcast.43), channel_id=1, source_target_pairs={{0,1},{1,0},{2,3},{3,2},{4,5},{5,4},{6,7},{7,6},{8,9},{9,8},{10,11... | collective-permute-start | bytes 3145736 | tf_op jit(solution)/shard_map/ppermute | solution.py:27
  192.1 1.6 collective-permute-done.29
  194.8 2.9 %collective-permute-start.30 = (f32[2,128,256]{2,1,0:T(8,128)S(1)}, f32[2,128,256]{2,1,0:T(8,128)S(1)}, u32[]{:S(2)}, u32[]{:S(2)}) collective-permute-start(f32[2,128,256]{2,1,0:T(8,128)S(1)} %broadcast_select_fusion), channel_id=1, source_target_pairs={{0,1},{1,0},{2,3},{3,2},{4,5},{5,4},{6,7},{7,6},{8,9},{9,8},{10,11... | collective-permute-start | bytes 786440 | tf_op jit(solution)/shard_map/ppermute | solution.py:27
  199.9 1.6 maximum_select_fusion
  (79 shorter events, 23.2 us)
Async XLA Ops:
  0.6 68.0 %collective-permute-start = (f32[2048,1024]{1,0:T(8,128)}, f32[2048,1024]{1,0:T(8,128)}, u32[]{:S(2)}, u32[]{:S(2)}) collective-permute-start(f32[2048,1024]{1,0:T(8,128)} %a.1), channel_id=1, source_target_pairs={{0,1},{1,0},{2,3},{3,2},{4,5},{5,4},{6,7},{7,6},{8,9},{9,8},{10,11... | collective-permute-start | bytes 25165832 | tf_op jit(solution)/shard_map/ppermute | solution.py:27
  22.3 15.1 %all-to-all-start.1 = ((f32[16,16,512]{2,1,0:T(8,128)}), f32[16,16,512]{2,1,0:T(8,128)S(1)}, u32[]{:S(2)}, u32[]{:S(2)}) async-start(f32[16,16,512]{2,1,0:T(8,128)} %bitcast.9), calls=%async_computation.1 | async-start | bytes 1048576 | tf_op jit(solution)/shard_map/all_to_all | solution.py:242
  37.6 15.5 %collective-permute-start.3 = (f32[8,16,512]{2,1,0:T(8,128)S(1)}, f32[8,16,512]{2,1,0:T(8,128)S(1)}, u32[]{:S(2)}, u32[]{:S(2)}) collective-permute-start(f32[8,16,512]{2,1,0:T(8,128)S(1)} %get-tuple-element.35), channel_id=1, source_target_pairs={{0,64},{1,65},{2,66},{3,67},{4,68},{5,69},{6,70},{7,71},{8,72},{9,... | collective-permute-start | bytes 786440 | tf_op jit(solution)/shard_map/ppermute | solution.py:43
  39.3 13.8 %collective-permute-start.4 = (f32[8,16,512]{2,1,0:T(8,128)S(1)}, f32[8,16,512]{2,1,0:T(8,128)S(1)}, u32[]{:S(2)}, u32[]{:S(2)}) collective-permute-start(f32[8,16,512]{2,1,0:T(8,128)S(1)} %get-tuple-element.35), channel_id=1, source_target_pairs={{0,96},{1,97},{2,98},{3,99},{4,100},{5,101},{6,102},{7,103},{8,104... | collective-permute-start | bytes 786440 | tf_op jit(solution)/shard_map/ppermute | solution.py:43
  40.5 12.7 %collective-permute-start.1 = (f32[8,16,512]{2,1,0:T(8,128)S(1)}, f32[8,16,512]{2,1,0:T(8,128)S(1)}, u32[]{:S(2)}, u32[]{:S(2)}) collective-permute-start(f32[8,16,512]{2,1,0:T(8,128)S(1)} %get-tuple-element.74), channel_id=1, source_target_pairs={{0,16},{1,17},{2,18},{3,19},{4,20},{5,21},{6,22},{7,23},{8,24},{9,... | collective-permute-start | bytes 786440 | tf_op jit(solution)/shard_map/ppermute | solution.py:35
  46.1 12.1 %collective-permute-start.21 = (f32[512,128]{1,0:T(8,128)S(1)}, f32[512,128]{1,0:T(8,128)S(1)}, u32[]{:S(2)}, u32[]{:S(2)}) collective-permute-start(f32[512,128]{1,0:T(8,128)S(1)} %bitcast.48), channel_id=1, source_target_pairs={{0,1},{1,0},{2,3},{3,2},{4,5},{5,4},{6,7},{7,6},{8,9},{9,8},{10,11... | collective-permute-start | bytes 786440 | tf_op jit(solution)/shard_map/ppermute | solution.py:27
  53.4 30.2 %collective-permute-start.16 = (f32[4,8,16,256]{3,2,1,0:T(8,128)S(1)}, f32[4,8,16,256]{3,2,1,0:T(8,128)S(1)}, u32[]{:S(2)}, u32[]{:S(2)}) collective-permute-start(f32[4,8,16,256]{3,2,1,0:T(8,128)S(1)} %get-tuple-element.62.rest_4_), channel_id=1, source_target_pairs={{0,16},{1,17},{2,18},{3,19},{4,20},{5,21},{6,22},{7,23},{8,24},{9,... | collective-permute-start | bytes 1572872 | tf_op jit(solution)/shard_map/ppermute | solution.py:35
  54.9 24.7 %collective-permute-start.13 = (f32[2,8,16,256]{3,2,1,0:T(8,128)S(1)}, f32[2,8,16,256]{3,2,1,0:T(8,128)S(1)}, u32[]{:S(2)}, u32[]{:S(2)}) collective-permute-start(f32[2,8,16,256]{3,2,1,0:T(8,128)S(1)} %get-tuple-element.70.rest_0_), channel_id=1, source_target_pairs={{0,32},{1,33},{2,34},{3,35},{4,36},{5,37},{6,38},{7,39},{8,40},{9,... | collective-permute-start | bytes 786440 | tf_op jit(solution)/shard_map/ppermute | solution.py:43
  55.1 26.0 %collective-permute-start.14 = (f32[2,8,16,256]{3,2,1,0:T(8,128)S(1)}, f32[2,8,16,256]{3,2,1,0:T(8,128)S(1)}, u32[]{:S(2)}, u32[]{:S(2)}) collective-permute-start(f32[2,8,16,256]{3,2,1,0:T(8,128)S(1)} %get-tuple-element.70.rest_0_), channel_id=1, source_target_pairs={{0,64},{1,65},{2,66},{3,67},{4,68},{5,69},{6,70},{7,71},{8,72},{9,... | collective-permute-start | bytes 786440 | tf_op jit(solution)/shard_map/ppermute | solution.py:43
  58.9 22.6 %collective-permute-start.15 = (f32[2,8,16,256]{3,2,1,0:T(8,128)S(1)}, f32[2,8,16,256]{3,2,1,0:T(8,128)S(1)}, u32[]{:S(2)}, u32[]{:S(2)}) collective-permute-start(f32[2,8,16,256]{3,2,1,0:T(8,128)S(1)} %get-tuple-element.70.rest_0_), channel_id=1, source_target_pairs={{0,96},{1,97},{2,98},{3,99},{4,100},{5,101},{6,102},{7,103},{8,104... | collective-permute-start | bytes 786440 | tf_op jit(solution)/shard_map/ppermute | solution.py:43
  68.7 36.5 %collective-permute-start.23 = (f32[512,128]{1,0:T(8,128)S(1)}, f32[512,128]{1,0:T(8,128)S(1)}, u32[]{:S(2)}, u32[]{:S(2)}) collective-permute-start(f32[512,128]{1,0:T(8,128)S(1)} %get-tuple-element.66.refs_14_), channel_id=1, source_target_pairs={{0,6},{1,7},{2,0},{3,1},{4,2},{5,3},{6,4},{7,5},{8,14},{9,15},{10,... | collective-permute-start | bytes 786440 | tf_op jit(solution)/shard_map/ppermute | solution.py:31
  79.7 14.3 %collective-permute-start.5 = (f32[2,8,16,256]{3,2,1,0:T(8,128)S(1)}, f32[2,8,16,256]{3,2,1,0:T(8,128)S(1)}, u32[]{:S(2)}, u32[]{:S(2)}) collective-permute-start(f32[2,8,16,256]{3,2,1,0:T(8,128)S(1)} %get-tuple-element.71.rest_0_), channel_id=1, source_target_pairs={{0,32},{1,33},{2,34},{3,35},{4,36},{5,37},{6,38},{7,39},{8,40},{9,... | collective-permute-start | bytes 786440 | tf_op jit(solution)/shard_map/ppermute | solution.py:43
  81.1 12.9 %collective-permute-start.6 = (f32[2,8,16,256]{3,2,1,0:T(8,128)S(1)}, f32[2,8,16,256]{3,2,1,0:T(8,128)S(1)}, u32[]{:S(2)}, u32[]{:S(2)}) collective-permute-start(f32[2,8,16,256]{3,2,1,0:T(8,128)S(1)} %get-tuple-element.71.rest_0_), channel_id=1, source_target_pairs={{0,64},{1,65},{2,66},{3,67},{4,68},{5,69},{6,70},{7,71},{8,72},{9,... | collective-permute-start | bytes 786440 | tf_op jit(solution)/shard_map/ppermute | solution.py:43
  81.5 12.6 %collective-permute-start.7 = (f32[2,8,16,256]{3,2,1,0:T(8,128)S(1)}, f32[2,8,16,256]{3,2,1,0:T(8,128)S(1)}, u32[]{:S(2)}, u32[]{:S(2)}) collective-permute-start(f32[2,8,16,256]{3,2,1,0:T(8,128)S(1)} %get-tuple-element.71.rest_0_), channel_id=1, source_target_pairs={{0,96},{1,97},{2,98},{3,99},{4,100},{5,101},{6,102},{7,103},{8,104... | collective-permute-start | bytes 786440 | tf_op jit(solution)/shard_map/ppermute | solution.py:43
  83.6 13.1 %collective-permute-start.8 = (f32[4,8,16,256]{3,2,1,0:T(8,128)S(1)}, f32[4,8,16,256]{3,2,1,0:T(8,128)S(1)}, u32[]{:S(2)}, u32[]{:S(2)}) collective-permute-start(f32[4,8,16,256]{3,2,1,0:T(8,128)S(1)} %get-tuple-element.63.rest_4_), channel_id=1, source_target_pairs={{0,16},{1,17},{2,18},{3,19},{4,20},{5,21},{6,22},{7,23},{8,24},{9,... | collective-permute-start | bytes 1572872 | tf_op jit(solution)/shard_map/ppermute | solution.py:35
  93.9 13.1 %collective-permute-start.24 = (f32[512,128]{1,0:T(8,128)S(1)}, f32[512,128]{1,0:T(8,128)S(1)}, u32[]{:S(2)}, u32[]{:S(2)}) collective-permute-start(f32[512,128]{1,0:T(8,128)S(1)} %get-tuple-element.66.refs_14_), channel_id=1, source_target_pairs={{0,4},{1,5},{2,6},{3,7},{4,0},{5,1},{6,2},{7,3},{8,12},{9,13},{10,... | collective-permute-start | bytes 786440 | tf_op jit(solution)/shard_map/ppermute | solution.py:31
  94.0 15.6 %collective-permute-start.25 = (f32[512,128]{1,0:T(8,128)S(1)}, f32[512,128]{1,0:T(8,128)S(1)}, u32[]{:S(2)}, u32[]{:S(2)}) collective-permute-start(f32[512,128]{1,0:T(8,128)S(1)} %get-tuple-element.66.refs_14_), channel_id=1, source_target_pairs={{0,2},{1,3},{2,4},{3,5},{4,6},{5,7},{6,0},{7,1},{8,10},{9,11},{10,... | collective-permute-start | bytes 786440 | tf_op jit(solution)/shard_map/ppermute | solution.py:31
  94.1 16.9 %collective-permute-start.22 = (f32[512,128]{1,0:T(8,128)S(1)}, f32[512,128]{1,0:T(8,128)S(1)}, u32[]{:S(2)}, u32[]{:S(2)}) collective-permute-start(f32[512,128]{1,0:T(8,128)S(1)} %get-tuple-element.67.refs_12_), channel_id=1, source_target_pairs={{0,8},{1,9},{2,10},{3,11},{4,12},{5,13},{6,14},{7,15},{8,0},{9,1},... | collective-permute-start | bytes 786440 | tf_op jit(solution)/shard_map/ppermute | solution.py:39
  96.7 18.9 %collective-permute-start.17 = (f32[2,128,256]{2,1,0:T(8,128)S(1)}, f32[2,128,256]{2,1,0:T(8,128)S(1)}, u32[]{:S(2)}, u32[]{:S(2)}) collective-permute-start(f32[2,128,256]{2,1,0:T(8,128)S(1)} %get-tuple-element.46), channel_id=1, source_target_pairs={{0,2},{1,3},{2,4},{3,5},{4,6},{5,7},{6,0},{7,1},{8,10},{9,11},{10,... | collective-permute-start | bytes 786440 | tf_op jit(solution)/shard_map/ppermute | solution.py:31
  105.2 10.4 %collective-permute-start.18 = (f32[2,128,256]{2,1,0:T(8,128)S(1)}, f32[2,128,256]{2,1,0:T(8,128)S(1)}, u32[]{:S(2)}, u32[]{:S(2)}) collective-permute-start(f32[2,128,256]{2,1,0:T(8,128)S(1)} %get-tuple-element.47), channel_id=1, source_target_pairs={{0,6},{1,7},{2,0},{3,1},{4,2},{5,3},{6,4},{7,5},{8,14},{9,15},{10,... | collective-permute-start | bytes 786440 | tf_op jit(solution)/shard_map/ppermute | solution.py:31
  107.0 12.1 %collective-permute-start.19 = (f32[2,128,256]{2,1,0:T(8,128)S(1)}, f32[2,128,256]{2,1,0:T(8,128)S(1)}, u32[]{:S(2)}, u32[]{:S(2)}) collective-permute-start(f32[2,128,256]{2,1,0:T(8,128)S(1)} %get-tuple-element.48), channel_id=1, source_target_pairs={{0,4},{1,5},{2,6},{3,7},{4,0},{5,1},{6,2},{7,3},{8,12},{9,13},{10,... | collective-permute-start | bytes 786440 | tf_op jit(solution)/shard_map/ppermute | solution.py:31
  109.7 20.9 %collective-permute-start.20 = (f32[4,128,256]{2,1,0:T(8,128)S(1)}, f32[4,128,256]{2,1,0:T(8,128)S(1)}, u32[]{:S(2)}, u32[]{:S(2)}) collective-permute-start(f32[4,128,256]{2,1,0:T(8,128)S(1)} %get-tuple-element.50), channel_id=1, source_target_pairs={{0,8},{1,9},{2,10},{3,11},{4,12},{5,13},{6,14},{7,15},{8,0},{9,1},... | collective-permute-start | bytes 1572872 | tf_op jit(solution)/shard_map/ppermute | solution.py:39
  111.1 22.9 %collective-permute-start.12 = (f32[4,128,256]{2,1,0:T(8,128)S(1)}, f32[4,128,256]{2,1,0:T(8,128)S(1)}, u32[]{:S(2)}, u32[]{:S(2)}) collective-permute-start(f32[4,128,256]{2,1,0:T(8,128)S(1)} %get-tuple-element.44), channel_id=1, source_target_pairs={{0,8},{1,9},{2,10},{3,11},{4,12},{5,13},{6,14},{7,15},{8,0},{9,1},... | collective-permute-start | bytes 1572872 | tf_op jit(solution)/shard_map/ppermute | solution.py:39
  115.6 9.7 %collective-permute-start.10 = (f32[2,128,256]{2,1,0:T(8,128)S(1)}, f32[2,128,256]{2,1,0:T(8,128)S(1)}, u32[]{:S(2)}, u32[]{:S(2)}) collective-permute-start(f32[2,128,256]{2,1,0:T(8,128)S(1)} %get-tuple-element.41), channel_id=1, source_target_pairs={{0,6},{1,7},{2,0},{3,1},{4,2},{5,3},{6,4},{7,5},{8,14},{9,15},{10,... | collective-permute-start | bytes 786440 | tf_op jit(solution)/shard_map/ppermute | solution.py:31
  119.1 11.5 %collective-permute-start.9 = (f32[2,128,256]{2,1,0:T(8,128)S(1)}, f32[2,128,256]{2,1,0:T(8,128)S(1)}, u32[]{:S(2)}, u32[]{:S(2)}) collective-permute-start(f32[2,128,256]{2,1,0:T(8,128)S(1)} %get-tuple-element.40), channel_id=1, source_target_pairs={{0,2},{1,3},{2,4},{3,5},{4,6},{5,7},{6,0},{7,1},{8,10},{9,11},{10,... | collective-permute-start | bytes 786440 | tf_op jit(solution)/shard_map/ppermute | solution.py:31
  137.0 25.8 %all-to-all-start.2 = ((f32[64,8,512]{2,1,0:T(8,128)}), f32[64,8,512]{2,1,0:T(8,128)S(1)}, u32[]{:S(2)}, u32[]{:S(2)}) async-start(f32[64,8,512]{2,1,0:T(8,128)} %bitcast.25), calls=%async_computation.2 | async-start | bytes 2097152 | tf_op jit(solution)/shard_map/all_to_all | solution.py:272
  164.7 21.8 %all-to-all-start.3 = ((f32[64,8,512]{2,1,0:T(8,128)}), f32[64,8,512]{2,1,0:T(8,128)S(1)}, u32[]{:S(2)}, u32[]{:S(2)}) async-start(f32[64,8,512]{2,1,0:T(8,128)} %broadcast_in_dim.9), calls=%async_computation.3 | async-start | bytes 2097152 | tf_op jit(solution)/shard_map/all_to_all | solution.py:276
  170.0 22.1 %collective-permute-start.26 = (f32[2,128,256]{2,1,0:T(8,128)S(1)}, f32[2,128,256]{2,1,0:T(8,128)S(1)}, u32[]{:S(2)}, u32[]{:S(2)}) collective-permute-start(f32[2,128,256]{2,1,0:T(8,128)S(1)} %get-tuple-element.52), channel_id=1, source_target_pairs={{0,8},{1,9},{2,10},{3,11},{4,12},{5,13},{6,14},{7,15},{8,0},{9,1},... | collective-permute-start | bytes 786440 | tf_op jit(solution)/shard_map/ppermute | solution.py:39
  171.0 21.0 %collective-permute-start.27 = (f32[2,128,256]{2,1,0:T(8,128)S(1)}, f32[2,128,256]{2,1,0:T(8,128)S(1)}, u32[]{:S(2)}, u32[]{:S(2)}) collective-permute-start(f32[2,128,256]{2,1,0:T(8,128)S(1)} %get-tuple-element.54), channel_id=1, source_target_pairs={{0,2},{1,3},{2,4},{3,5},{4,6},{5,7},{6,0},{7,1},{8,10},{9,11},{10,... | collective-permute-start | bytes 786440 | tf_op jit(solution)/shard_map/ppermute | solution.py:31
  172.2 19.8 %collective-permute-start.28 = (f32[2,128,256]{2,1,0:T(8,128)S(1)}, f32[2,128,256]{2,1,0:T(8,128)S(1)}, u32[]{:S(2)}, u32[]{:S(2)}) collective-permute-start(f32[2,128,256]{2,1,0:T(8,128)S(1)} %get-tuple-element.55), channel_id=1, source_target_pairs={{0,6},{1,7},{2,0},{3,1},{4,2},{5,3},{6,4},{7,5},{8,14},{9,15},{10,... | collective-permute-start | bytes 786440 | tf_op jit(solution)/shard_map/ppermute | solution.py:31
  173.7 20.0 %collective-permute-start.29 = (f32[2,128,256]{2,1,0:T(8,128)S(1)}, f32[2,128,256]{2,1,0:T(8,128)}, u32[]{:S(2)}, u32[]{:S(2)}) collective-permute-start(f32[2,128,256]{2,1,0:T(8,128)S(1)} %get-tuple-element.56), channel_id=1, source_target_pairs={{0,4},{1,5},{2,6},{3,7},{4,0},{5,1},{6,2},{7,3},{8,12},{9,13},{10,... | collective-permute-start | bytes 786440 | tf_op jit(solution)/shard_map/ppermute | solution.py:31
  186.5 13.3 %collective-permute-start.31 = (f32[512,512]{1,0:T(8,128)S(1)}, f32[512,512]{1,0:T(8,128)S(1)}, u32[]{:S(2)}, u32[]{:S(2)}) collective-permute-start(f32[512,512]{1,0:T(8,128)S(1)} %bitcast.43), channel_id=1, source_target_pairs={{0,1},{1,0},{2,3},{3,2},{4,5},{5,4},{6,7},{7,6},{8,9},{9,8},{10,11... | collective-permute-start | bytes 3145736 | tf_op jit(solution)/shard_map/ppermute | solution.py:27
  (8 other events, 114.5 us)

commit v2 on v1

--- a/solution.py
+++ b/solution.py
@@ -48,32 +48,7 @@
     return hi, (a - hi.astype(jnp.float32)).astype(jnp.bfloat16)
 
 
-def prepare_kernel(a, hi, lo):
-    def step(a, hi, lo):
-        hi[...], lo[...] = halves(a[...])
-
-    spec = pl.BlockSpec((256, a.shape[1]), lambda i: (i, 0))
-    pltpu.emit_pipeline(
-        step, grid=(a.shape[0] // 256,), in_specs=[spec], out_specs=[spec, spec]
-    )(a, hi, lo)
-
-
-def prepare(a):
-    spec = pl.BlockSpec(memory_space=pltpu.HBM)
-    out = jax.ShapeDtypeStruct(a.shape, jnp.bfloat16)
-    return pl.pallas_call(
-        prepare_kernel,
-        in_specs=[spec],
-        out_specs=[spec, spec],
-        out_shape=[out, out],
-        compiler_params=pltpu.CompilerParams(vmem_limit_bytes=54 << 20),
-        cost_estimate=pl.CostEstimate(
-            flops=4 * a.size, bytes_accessed=8 * a.size, transcendentals=0
-        ),
-    )(a)
-
-
-def panel_kernel(info, own_hi, own_lo, oth_hi, oth_lo, *rest):
+def panel_kernel(info, own, oth, *rest):
     (f0, f1, f2, f3, g_own, g_oth), outs, (f_hi, f_lo, acc) = rest[:6], rest[6:12], rest[12:]
     core, z, yh, x, yl = info[8], info[9], info[10], info[11], info[12]
 
@@ -100,18 +75,18 @@
                     place(ref[s, col], col + 8, from_z * 2 + from_yh)
 
     acc[...] = jnp.zeros_like(acc)
-    for a_hi, a_lo, side in ((own_hi, own_lo, core), (oth_hi, oth_lo, 1 - core)):
+    for ref, side in ((own, core), (oth, 1 - core)):
         for j in range(2):
             tile = side * 2 + j
 
             @pl.when((info[i] > 0) & (info[4 + tile] > 0))
             def _():
                 at = pl.ds(pl.multiple_of(tile * TILE, TILE), TILE)
-                cols = slice(j * TILE, (j + 1) * TILE)
-                hi, b_hi = a_hi[:, cols], f_hi[at, :]
+                hi, lo = halves(ref[:, j * TILE : (j + 1) * TILE])
+                b_hi = f_hi[at, :]
                 acc[...] += (
                     jnp.dot(hi, b_hi, preferred_element_type=jnp.float32)
-                    + jnp.dot(a_lo[:, cols], b_hi, preferred_element_type=jnp.float32)
+                    + jnp.dot(lo, b_hi, preferred_element_type=jnp.float32)
                     + jnp.dot(hi, f_lo[at, :], preferred_element_type=jnp.float32)
                 )
 
@@ -139,10 +114,10 @@
     return [pl.BlockSpec(memory_space=pltpu.VMEM)] * n
 
 
-def panel(info, sides, pieces):
+def panel(info, own, oth, pieces):
     cols = pieces[0].shape[-1]
     whole = lambda v: pl.BlockSpec(v.shape, lambda i, info: (0,) * len(v.shape))
-    block = pl.BlockSpec((TILE, sides[0].shape[1]), lambda i, info: (info[13 + i], 0))
+    block = pl.BlockSpec((TILE, own.shape[1]), lambda i, info: (info[13 + i], 0))
     out = [jax.ShapeDtypeStruct((2, 128, cols), jnp.float32)] * 4
     out += [jax.ShapeDtypeStruct((4, 128, cols), jnp.float32)] * 2
     return pl.pallas_call(
@@ -150,7 +125,7 @@
         grid_spec=pltpu.PrefetchScalarGridSpec(
             num_scalar_prefetch=1,
             grid=(4,),
-            in_specs=[block] * 4 + [whole(v) for v in pieces],
+            in_specs=[block] * 2 + [whole(v) for v in pieces],
             out_specs=[whole(v) for v in out],
             scratch_shapes=[
                 pltpu.VMEM((2048, cols), jnp.bfloat16),
@@ -165,7 +140,7 @@
             bytes_accessed=20 << 20,
             transcendentals=0,
         ),
-    )(info, *sides, *pieces)
+    )(info, own, oth, *pieces)
 
 
 def finish_kernel(info, *refs):
@@ -228,8 +203,6 @@
     )
 
     oth = to_core(ancestor)
-    sides = prepare(ancestor)
-    sides = [*sides, *prepare(oth)]
 
     turned = jnp.swapaxes(factor, 1, 2)
     f_keep = pick(turned, core)
@@ -256,7 +229,7 @@
     parts = []
     for c in range(2):
         first0, first1, first2, first3, last_keep, last_send = panel(
-            info, sides, gathered[c]
+            info, ancestor, oth, gathered[c]
         )
         got = [to_x(first1, 1), to_x(first3, 3), to_x(first2, 2)]
         parts += [first0, *got, last_keep, to_yl(last_send)]

time: 202 us -> 194 us (0.960)
  Pallas kernels: 38.1 us -> 19.7 us
  waiting for transfers between devices: 65.3 us -> 72.6 us
  starting transfers between devices: 69.4 us -> 71.5 us
    pallas_call x2 -> x0, Pallas kernels: 18.6 us -> none  [prepare(): pl.pallas_call(prepare_kernel, in_specs=[spec], out_specs=[spec, spec], o...]
    ppermute x9, waiting for transfers between devices: 4.39 us -> 12.8 us  [to_z(): return lax.ppermute(v, AXES, route(lambda z, y, x, c: (z + s, y, x, c)))]
  transfers between devices with their start and end apart: 35 -> 35, of which waited for: 11 -> 14; matrix products, arithmetic and copies ran while one was open for 2% -> 3% of each run, Pallas kernels for 17% -> 9%
where the time goes in v2:
time: 194 us; the launch traced here: 193 us
  waiting for transfers between devices  72.6 us (37%)
  starting transfers between devices  71.5 us (37%)
  Pallas kernels  19.7 us (10%)
  blocking collectives  19.1 us (10%)
  other arithmetic  6.82 us (4%)
  local copies, waits for them, and re-layouts  2.88 us (1%)
    all_to_all x1, blocking collectives, per_device(): spread = lax.all_to_all(factor.reshape(2, 8, 16, WIDTH), ROW, 1, 0)  19.1 us
    all_to_all x1, waiting for transfers between devices, per_device(): diag = lax.all_to_all(diag.reshape(64, 8, WIDTH), CHIPS, 0, 0)  17.4 us
    ppermute x12, waiting for transfers between devices, to_x(): return lax.ppermute(v, AXES, route(lambda z, y, x, c: (z, y, x + s, c)))  17.3 us
    ppermute x4, starting transfers between devices, to_core(): return lax.ppermute(v, AXES, route(lambda z, y, x, c: (z, y, x, 1 - c)))  16.9 us
    pallas_call x2, Pallas kernels, panel(): pl.pallas_call(panel_kernel, grid_spec=pltpu.PrefetchScalarGridSpec(num_s...  16.6 us
    ppermute x12, starting transfers between devices, to_x(): return lax.ppermute(v, AXES, route(lambda z, y, x, c: (z, y, x + s, c)))  15.1 us
    ppermute x9, waiting for transfers between devices, to_z(): return lax.ppermute(v, AXES, route(lambda z, y, x, c: (z + s, y, x, c)))  12.8 us
    all_to_all x1, waiting for transfers between devices, per_device(): diag = lax.all_to_all(jnp.broadcast_to(diag, (64, 8, WIDTH)), CHIPS, 0, 0)  11.3 us
  transfers between devices with their start and end apart: 35, of which 14 were waited for; matrix products, arithmetic and copies ran while one was open for 3% of the time, Pallas kernels for 9%

profile of v2, /device:TPU:1, one launch (start us, length us, event | category | flops | bytes accessed | tf_op | source)
XLA Modules:
  0.0 193.4 jit_solution(4238701281478024557)
XLA Ops:
  3.3 19.1 %all_to_all.30 = f32[1,2,8,16,512]{4,3,1,0,2:T(8,128)} all-to-all(f32[1,2,8,16,512]{4,3,1,0,2:T(8,128)S(1)} %copy.17), channel_id=1, replica_groups=mesh['z'=4,'yh'=2,'yl'=2,'x'=4,'core'=2] {'z','yh'}, dimensions={2} | all-to-all | bytes 1048576 | tf_op jit(solution)/shard_map/all_to_all | solution.py:214
  22.3 5.6 %all-to-all-start.1 = ((f32[16,16,512]{2,1,0:T(8,128)}), f32[16,16,512]{2,1,0:T(8,128)S(1)}, u32[]{:S(2)}, u32[]{:S(2)}) async-start(f32[16,16,512]{2,1,0:T(8,128)} %bitcast.9), calls=%async_computation.1 | async-start | bytes 1048576 | tf_op jit(solution)/shard_map/all_to_all | solution.py:215
  27.9 9.5 %all-to-all-done.1 = f32[16,16,512]{2,1,0:T(8,128)S(1)} async-done(((f32[16,16,512]{2,1,0:T(8,128)}), f32[16,16,512]{2,1,0:T(8,128)S(1)}, u32[]{:S(2)}, u32[]{:S(2)}) %all-to-all-start.1) | async-done | bytes 524320 | tf_op jit(solution)/shard_map/all_to_all | solution.py:215
  37.6 1.7 collective-permute-start.3
  41.7 4.4 %collective-permute-done.2 = f32[8,16,512]{2,1,0:T(8,128)S(1)} collective-permute-done((f32[8,16,512]{2,1,0:T(8,128)S(1)}, f32[8,16,512]{2,1,0:T(8,128)S(1)}, u32[]{:S(2)}, u32[]{:S(2)}) %collective-permute-start.2) | collective-permute-done | bytes 262176 | tf_op jit(solution)/shard_map/ppermute | solution.py:43
  46.1 7.0 %collective-permute-start.21 = (f32[512,128]{1,0:T(8,128)S(1)}, f32[512,128]{1,0:T(8,128)}, u32[]{:S(2)}, u32[]{:S(2)}) collective-permute-start(f32[512,128]{1,0:T(8,128)S(1)} %bitcast.48), channel_id=1, source_target_pairs={{0,1},{1,0},{2,3},{3,2},{4,5},{5,4},{6,7},{7,6},{8,9},{9,8},{10,11... | collective-permute-start | bytes 786440 | tf_op jit(solution)/shard_map/ppermute | solution.py:27
  56.1 3.1 %collective-permute-start.14 = (f32[2,8,16,256]{3,2,1,0:T(8,128)S(1)}, f32[2,8,16,256]{3,2,1,0:T(8,128)S(1)}, u32[]{:S(2)}, u32[]{:S(2)}) collective-permute-start(f32[2,8,16,256]{3,2,1,0:T(8,128)S(1)} %get-tuple-element.62.rest_0_), channel_id=1, source_target_pairs={{0,64},{1,65},{2,66},{3,67},{4,68},{5,69},{6,70},{7,71},{8,72},{9,... | collective-permute-start | bytes 786440 | tf_op jit(solution)/shard_map/ppermute | solution.py:43
  60.5 3.6 %collective-permute-done.13.rest_1_ = f32[2,8,16,256]{3,2,1,0:T(8,128)S(1)} collective-permute-done((f32[2,8,16,256]{3,2,1,0:T(8,128)S(1)}, f32[2,8,16,256]{3,2,1,0:T(8,128)S(1)}, u32[]{:S(2)}, u32[]{:S(2)}) %collective-permute-start.13) | collective-permute-done | bytes 262176 | tf_op jit(solution)/shard_map/ppermute | solution.py:43
  64.1 1.6 collective-permute-start.23
  65.7 4.5 %collective-permute-done.14.rest_2_ = f32[2,8,16,256]{3,2,1,0:T(8,128)S(1)} collective-permute-done((f32[2,8,16,256]{3,2,1,0:T(8,128)S(1)}, f32[2,8,16,256]{3,2,1,0:T(8,128)S(1)}, u32[]{:S(2)}, u32[]{:S(2)}) %collective-permute-start.14) | collective-permute-done | bytes 262176 | tf_op jit(solution)/shard_map/ppermute | solution.py:43
  71.2 2.8 %collective-permute-start.7 = (f32[2,8,16,256]{3,2,1,0:T(8,128)S(1)}, f32[2,8,16,256]{3,2,1,0:T(8,128)S(1)}, u32[]{:S(2)}, u32[]{:S(2)}) collective-permute-start(f32[2,8,16,256]{3,2,1,0:T(8,128)S(1)} %get-tuple-element.63.rest_0_), channel_id=1, source_target_pairs={{0,96},{1,97},{2,98},{3,99},{4,100},{5,101},{6,102},{7,103},{8,104... | collective-permute-start | bytes 786440 | tf_op jit(solution)/shard_map/ppermute | solution.py:43
  74.0 1.8 collective-permute-start.8
  75.8 8.3 %shard_map.60 = (f32[2,128,256]{2,1,0:T(8,128)S(1)}, f32[2,128,256]{2,1,0:T(8,128)S(1)}, f32[2,128,256]{2,1,0:T(8,128)S(1)}, f32[2,128,256]{2,1,0:T(8,128)S(1)},...) custom-call(s32[17]{0:T(128)S(1)} %concatenate.6.info, f32[2048,1024]{1,0:T(8,128)} %own.3, ...), custom_call_target="tpu_custom_call" | custom-call | flops 6442450944 | bytes 20971520 | tf_op jit(solution)/shard_map/pallas_call | solution.py:123
  85.8 2.0 %collective-permute-start.22 = (f32[512,128]{1,0:T(8,128)S(1)}, f32[512,128]{1,0:T(8,128)S(1)}, u32[]{:S(2)}, u32[]{:S(2)}) collective-permute-start(f32[512,128]{1,0:T(8,128)S(1)} %get-tuple-element.59.refs_12_), channel_id=1, source_target_pairs={{0,8},{1,9},{2,10},{3,11},{4,12},{5,13},{6,14},{7,15},{8,0},{9,1},... | collective-permute-start | bytes 786440 | tf_op jit(solution)/shard_map/ppermute | solution.py:39
  88.2 8.3 %shard_map.59 = (f32[2,128,256]{2,1,0:T(8,128)S(1)}, f32[2,128,256]{2,1,0:T(8,128)S(1)}, f32[2,128,256]{2,1,0:T(8,128)S(1)}, f32[2,128,256]{2,1,0:T(8,128)S(1)},...) custom-call(s32[17]{0:T(128)S(1)} %concatenate.6.info, f32[2048,1024]{1,0:T(8,128)} %own.3, ...), custom_call_target="tpu_custom_call" | custom-call | flops 6442450944 | bytes 20971520 | tf_op jit(solution)/shard_map/pallas_call | solution.py:123
  96.5 1.6 collective-permute-start.18
  98.1 2.0 %collective-permute-start.19 = (f32[2,128,256]{2,1,0:T(8,128)S(1)}, f32[2,128,256]{2,1,0:T(8,128)S(1)}, u32[]{:S(2)}, u32[]{:S(2)}) collective-permute-start(f32[2,128,256]{2,1,0:T(8,128)S(1)} %get-tuple-element.40), channel_id=1, source_target_pairs={{0,4},{1,5},{2,6},{3,7},{4,0},{5,1},{6,2},{7,3},{8,12},{9,13},{10,... | collective-permute-start | bytes 786440 | tf_op jit(solution)/shard_map/ppermute | solution.py:31
  101.6 5.4 %collective-permute-done.17.refs_7_ = f32[2,128,256]{2,1,0:T(8,128)S(1)} collective-permute-done((f32[2,128,256]{2,1,0:T(8,128)S(1)}, f32[2,128,256]{2,1,0:T(8,128)S(1)}, u32[]{:S(2)}, u32[]{:S(2)}) %collective-permute-start.17) | collective-permute-done | bytes 262176 | tf_op jit(solution)/shard_map/ppermute | solution.py:31
  109.0 3.2 %collective-permute-start.9 = (f32[2,128,256]{2,1,0:T(8,128)S(1)}, f32[2,128,256]{2,1,0:T(8,128)S(1)}, u32[]{:S(2)}, u32[]{:S(2)}) collective-permute-start(f32[2,128,256]{2,1,0:T(8,128)S(1)} %get-tuple-element.32), channel_id=1, source_target_pairs={{0,2},{1,3},{2,4},{3,5},{4,6},{5,7},{6,0},{7,1},{8,10},{9,11},{10,... | collective-permute-start | bytes 786440 | tf_op jit(solution)/shard_map/ppermute | solution.py:31
  112.2 3.8 %collective-permute-done.10.refs_2_ = f32[2,128,256]{2,1,0:T(8,128)S(1)} collective-permute-done((f32[2,128,256]{2,1,0:T(8,128)S(1)}, f32[2,128,256]{2,1,0:T(8,128)S(1)}, u32[]{:S(2)}, u32[]{:S(2)}) %collective-permute-start.10) | collective-permute-done | bytes 262176 | tf_op jit(solution)/shard_map/ppermute | solution.py:31
  115.9 5.1 %collective-permute-done.9.refs_1_ = f32[2,128,256]{2,1,0:T(8,128)S(1)} collective-permute-done((f32[2,128,256]{2,1,0:T(8,128)S(1)}, f32[2,128,256]{2,1,0:T(8,128)S(1)}, u32[]{:S(2)}, u32[]{:S(2)}) %collective-permute-start.9) | collective-permute-done | bytes 262176 | tf_op jit(solution)/shard_map/ppermute | solution.py:31
  121.0 3.1 %collective-permute-done.12.refs_5_ = f32[4,128,256]{2,1,0:T(8,128)S(1)} collective-permute-done((f32[4,128,256]{2,1,0:T(8,128)S(1)}, f32[4,128,256]{2,1,0:T(8,128)S(1)}, u32[]{:S(2)}, u32[]{:S(2)}) %collective-permute-start.12) | collective-permute-done | bytes 524320 | tf_op jit(solution)/shard_map/ppermute | solution.py:39
  124.1 3.1 %shard_map.61 = (f32[512,512]{1,0:T(8,128)}, f32[2,128,256]{2,1,0:T(8,128)S(1)}, f32[2,128,256]{2,1,0:T(8,128)S(1)}, f32[2,128,256]{2,1,0:T(8,128)S(1)}, f32[2,1...) custom-call(s32[17]{0:T(128)S(1)} %concatenate.6.info, ...), custom_call_target="tpu_custom_call" | custom-call | flops 1207959552 | bytes 9437184 | tf_op jit(solution)/shard_map/pallas_call | solution.py:169
  127.2 10.3 %all-to-all-start.2 = ((f32[64,8,512]{2,1,0:T(8,128)}), f32[64,8,512]{2,1,0:T(8,128)S(1)}, u32[]{:S(2)}, u32[]{:S(2)}) async-start(f32[64,8,512]{2,1,0:T(8,128)} %bitcast.25), calls=%async_computation.2 | async-start | bytes 2097152 | tf_op jit(solution)/shard_map/all_to_all | solution.py:245
  137.5 17.4 %all-to-all-done.2 = f32[64,8,512]{2,1,0:T(8,128)S(1)} async-done(((f32[64,8,512]{2,1,0:T(8,128)}), f32[64,8,512]{2,1,0:T(8,128)S(1)}, u32[]{:S(2)}, u32[]{:S(2)}) %all-to-all-start.2) | async-done | bytes 1048608 | tf_op jit(solution)/shard_map/all_to_all | solution.py:245
  156.8 5.2 %all-to-all-start.3 = ((f32[64,8,512]{2,1,0:T(8,128)}), f32[64,8,512]{2,1,0:T(8,128)S(1)}, u32[]{:S(2)}, u32[]{:S(2)}) async-start(f32[64,8,512]{2,1,0:T(8,128)} %broadcast_in_dim.9), calls=%async_computation.3 | async-start | bytes 2097152 | tf_op jit(solution)/shard_map/all_to_all | solution.py:249
  164.3 1.5 collective-permute-start.28
  167.3 11.3 %all-to-all-done.3 = f32[64,8,512]{2,1,0:T(8,128)S(1)} async-done(((f32[64,8,512]{2,1,0:T(8,128)}), f32[64,8,512]{2,1,0:T(8,128)S(1)}, u32[]{:S(2)}, u32[]{:S(2)}) %all-to-all-start.3) | async-done | bytes 1048608 | tf_op jit(solution)/shard_map/all_to_all | solution.py:249
  178.6 5.5 %collective-permute-start.31 = (f32[512,512]{1,0:T(8,128)S(1)}, f32[512,512]{1,0:T(8,128)S(1)}, u32[]{:S(2)}, u32[]{:S(2)}) collective-permute-start(f32[512,512]{1,0:T(8,128)S(1)} %bitcast.43), channel_id=1, source_target_pairs={{0,1},{1,0},{2,3},{3,2},{4,5},{5,4},{6,7},{7,6},{8,9},{9,8},{10,11... | collective-permute-start | bytes 3145736 | tf_op jit(solution)/shard_map/ppermute | solution.py:27
  184.1 1.6 collective-permute-done.29
  186.9 2.9 %collective-permute-start.30 = (f32[2,128,256]{2,1,0:T(8,128)S(1)}, f32[2,128,256]{2,1,0:T(8,128)S(1)}, u32[]{:S(2)}, u32[]{:S(2)}) collective-permute-start(f32[2,128,256]{2,1,0:T(8,128)S(1)} %broadcast_select_fusion), channel_id=1, source_target_pairs={{0,1},{1,0},{2,3},{3,2},{4,5},{5,4},{6,7},{7,6},{8,9},{9,8},{10,11... | collective-permute-start | bytes 786440 | tf_op jit(solution)/shard_map/ppermute | solution.py:27
  191.9 1.6 maximum_select_fusion
  (73 shorter events, 24.7 us)
Async XLA Ops:
  0.6 73.3 %collective-permute-start = (f32[2048,1024]{1,0:T(8,128)}, f32[2048,1024]{1,0:T(8,128)}, u32[]{:S(2)}, u32[]{:S(2)}) collective-permute-start(f32[2048,1024]{1,0:T(8,128)} %own.3), channel_id=1, source_target_pairs={{0,1},{1,0},{2,3},{3,2},{4,5},{5,4},{6,7},{7,6},{8,9},{9,8},{10,11... | collective-permute-start | bytes 25165832 | tf_op jit(solution)/shard_map/ppermute | solution.py:27
  22.3 15.1 %all-to-all-start.1 = ((f32[16,16,512]{2,1,0:T(8,128)}), f32[16,16,512]{2,1,0:T(8,128)S(1)}, u32[]{:S(2)}, u32[]{:S(2)}) async-start(f32[16,16,512]{2,1,0:T(8,128)} %bitcast.9), calls=%async_computation.1 | async-start | bytes 1048576 | tf_op jit(solution)/shard_map/all_to_all | solution.py:215
  37.6 15.5 %collective-permute-start.3 = (f32[8,16,512]{2,1,0:T(8,128)S(1)}, f32[8,16,512]{2,1,0:T(8,128)S(1)}, u32[]{:S(2)}, u32[]{:S(2)}) collective-permute-start(f32[8,16,512]{2,1,0:T(8,128)S(1)} %get-tuple-element.27), channel_id=1, source_target_pairs={{0,64},{1,65},{2,66},{3,67},{4,68},{5,69},{6,70},{7,71},{8,72},{9,... | collective-permute-start | bytes 786440 | tf_op jit(solution)/shard_map/ppermute | solution.py:43
  39.3 13.8 %collective-permute-start.4 = (f32[8,16,512]{2,1,0:T(8,128)S(1)}, f32[8,16,512]{2,1,0:T(8,128)S(1)}, u32[]{:S(2)}, u32[]{:S(2)}) collective-permute-start(f32[8,16,512]{2,1,0:T(8,128)S(1)} %get-tuple-element.27), channel_id=1, source_target_pairs={{0,96},{1,97},{2,98},{3,99},{4,100},{5,101},{6,102},{7,103},{8,104... | collective-permute-start | bytes 786440 | tf_op jit(solution)/shard_map/ppermute | solution.py:43
  40.5 12.7 %collective-permute-start.1 = (f32[8,16,512]{2,1,0:T(8,128)S(1)}, f32[8,16,512]{2,1,0:T(8,128)S(1)}, u32[]{:S(2)}, u32[]{:S(2)}) collective-permute-start(f32[8,16,512]{2,1,0:T(8,128)S(1)} %get-tuple-element.66), channel_id=1, source_target_pairs={{0,16},{1,17},{2,18},{3,19},{4,20},{5,21},{6,22},{7,23},{8,24},{9,... | collective-permute-start | bytes 786440 | tf_op jit(solution)/shard_map/ppermute | solution.py:35
  46.1 13.1 %collective-permute-start.21 = (f32[512,128]{1,0:T(8,128)S(1)}, f32[512,128]{1,0:T(8,128)}, u32[]{:S(2)}, u32[]{:S(2)}) collective-permute-start(f32[512,128]{1,0:T(8,128)S(1)} %bitcast.48), channel_id=1, source_target_pairs={{0,1},{1,0},{2,3},{3,2},{4,5},{5,4},{6,7},{7,6},{8,9},{9,8},{10,11... | collective-permute-start | bytes 786440 | tf_op jit(solution)/shard_map/ppermute | solution.py:27
  53.4 17.8 %collective-permute-start.16 = (f32[4,8,16,256]{3,2,1,0:T(8,128)S(1)}, f32[4,8,16,256]{3,2,1,0:T(8,128)S(1)}, u32[]{:S(2)}, u32[]{:S(2)}) collective-permute-start(f32[4,8,16,256]{3,2,1,0:T(8,128)S(1)} %get-tuple-element.54.rest_4_), channel_id=1, source_target_pairs={{0,16},{1,17},{2,18},{3,19},{4,20},{5,21},{6,22},{7,23},{8,24},{9,... | collective-permute-start | bytes 1572872 | tf_op jit(solution)/shard_map/ppermute | solution.py:35
  56.1 14.1 %collective-permute-start.14 = (f32[2,8,16,256]{3,2,1,0:T(8,128)S(1)}, f32[2,8,16,256]{3,2,1,0:T(8,128)S(1)}, u32[]{:S(2)}, u32[]{:S(2)}) collective-permute-start(f32[2,8,16,256]{3,2,1,0:T(8,128)S(1)} %get-tuple-element.62.rest_0_), channel_id=1, source_target_pairs={{0,64},{1,65},{2,66},{3,67},{4,68},{5,69},{6,70},{7,71},{8,72},{9,... | collective-permute-start | bytes 786440 | tf_op jit(solution)/shard_map/ppermute | solution.py:43
  59.2 11.4 %collective-permute-start.15 = (f32[2,8,16,256]{3,2,1,0:T(8,128)S(1)}, f32[2,8,16,256]{3,2,1,0:T(8,128)S(1)}, u32[]{:S(2)}, u32[]{:S(2)}) collective-permute-start(f32[2,8,16,256]{3,2,1,0:T(8,128)S(1)} %get-tuple-element.62.rest_0_), channel_id=1, source_target_pairs={{0,96},{1,97},{2,98},{3,99},{4,100},{5,101},{6,102},{7,103},{8,104... | collective-permute-start | bytes 786440 | tf_op jit(solution)/shard_map/ppermute | solution.py:43
  64.1 32.4 %collective-permute-start.23 = (f32[512,128]{1,0:T(8,128)S(1)}, f32[512,128]{1,0:T(8,128)S(1)}, u32[]{:S(2)}, u32[]{:S(2)}) collective-permute-start(f32[512,128]{1,0:T(8,128)S(1)} %get-tuple-element.58.refs_14_), channel_id=1, source_target_pairs={{0,6},{1,7},{2,0},{3,1},{4,2},{5,3},{6,4},{7,5},{8,14},{9,15},{10,... | collective-permute-start | bytes 786440 | tf_op jit(solution)/shard_map/ppermute | solution.py:31
  70.2 13.9 %collective-permute-start.5 = (f32[2,8,16,256]{3,2,1,0:T(8,128)S(1)}, f32[2,8,16,256]{3,2,1,0:T(8,128)S(1)}, u32[]{:S(2)}, u32[]{:S(2)}) collective-permute-start(f32[2,8,16,256]{3,2,1,0:T(8,128)S(1)} %get-tuple-element.63.rest_0_), channel_id=1, source_target_pairs={{0,32},{1,33},{2,34},{3,35},{4,36},{5,37},{6,38},{7,39},{8,40},{9,... | collective-permute-start | bytes 786440 | tf_op jit(solution)/shard_map/ppermute | solution.py:43
  70.6 14.4 %collective-permute-start.6 = (f32[2,8,16,256]{3,2,1,0:T(8,128)S(1)}, f32[2,8,16,256]{3,2,1,0:T(8,128)S(1)}, u32[]{:S(2)}, u32[]{:S(2)}) collective-permute-start(f32[2,8,16,256]{3,2,1,0:T(8,128)S(1)} %get-tuple-element.63.rest_0_), channel_id=1, source_target_pairs={{0,64},{1,65},{2,66},{3,67},{4,68},{5,69},{6,70},{7,71},{8,72},{9,... | collective-permute-start | bytes 786440 | tf_op jit(solution)/shard_map/ppermute | solution.py:43
  71.2 14.6 %collective-permute-start.7 = (f32[2,8,16,256]{3,2,1,0:T(8,128)S(1)}, f32[2,8,16,256]{3,2,1,0:T(8,128)S(1)}, u32[]{:S(2)}, u32[]{:S(2)}) collective-permute-start(f32[2,8,16,256]{3,2,1,0:T(8,128)S(1)} %get-tuple-element.63.rest_0_), channel_id=1, source_target_pairs={{0,96},{1,97},{2,98},{3,99},{4,100},{5,101},{6,102},{7,103},{8,104... | collective-permute-start | bytes 786440 | tf_op jit(solution)/shard_map/ppermute | solution.py:43
  74.0 13.7 %collective-permute-start.8 = (f32[4,8,16,256]{3,2,1,0:T(8,128)S(1)}, f32[4,8,16,256]{3,2,1,0:T(8,128)S(1)}, u32[]{:S(2)}, u32[]{:S(2)}) collective-permute-start(f32[4,8,16,256]{3,2,1,0:T(8,128)S(1)} %get-tuple-element.55.rest_4_), channel_id=1, source_target_pairs={{0,16},{1,17},{2,18},{3,19},{4,20},{5,21},{6,22},{7,23},{8,24},{9,... | collective-permute-start | bytes 1572872 | tf_op jit(solution)/shard_map/ppermute | solution.py:35
  84.1 14.0 %collective-permute-start.24 = (f32[512,128]{1,0:T(8,128)S(1)}, f32[512,128]{1,0:T(8,128)S(1)}, u32[]{:S(2)}, u32[]{:S(2)}) collective-permute-start(f32[512,128]{1,0:T(8,128)S(1)} %get-tuple-element.58.refs_14_), channel_id=1, source_target_pairs={{0,4},{1,5},{2,6},{3,7},{4,0},{5,1},{6,2},{7,3},{8,12},{9,13},{10,... | collective-permute-start | bytes 786440 | tf_op jit(solution)/shard_map/ppermute | solution.py:31
  84.9 15.2 %collective-permute-start.25 = (f32[512,128]{1,0:T(8,128)S(1)}, f32[512,128]{1,0:T(8,128)S(1)}, u32[]{:S(2)}, u32[]{:S(2)}) collective-permute-start(f32[512,128]{1,0:T(8,128)S(1)} %get-tuple-element.58.refs_14_), channel_id=1, source_target_pairs={{0,2},{1,3},{2,4},{3,5},{4,6},{5,7},{6,0},{7,1},{8,10},{9,11},{10,... | collective-permute-start | bytes 786440 | tf_op jit(solution)/shard_map/ppermute | solution.py:31
  85.8 15.8 %collective-permute-start.22 = (f32[512,128]{1,0:T(8,128)S(1)}, f32[512,128]{1,0:T(8,128)S(1)}, u32[]{:S(2)}, u32[]{:S(2)}) collective-permute-start(f32[512,128]{1,0:T(8,128)S(1)} %get-tuple-element.59.refs_12_), channel_id=1, source_target_pairs={{0,8},{1,9},{2,10},{3,11},{4,12},{5,13},{6,14},{7,15},{8,0},{9,1},... | collective-permute-start | bytes 786440 | tf_op jit(solution)/shard_map/ppermute | solution.py:39
  87.7 19.3 %collective-permute-start.17 = (f32[2,128,256]{2,1,0:T(8,128)S(1)}, f32[2,128,256]{2,1,0:T(8,128)S(1)}, u32[]{:S(2)}, u32[]{:S(2)}) collective-permute-start(f32[2,128,256]{2,1,0:T(8,128)S(1)} %get-tuple-element.38), channel_id=1, source_target_pairs={{0,2},{1,3},{2,4},{3,5},{4,6},{5,7},{6,0},{7,1},{8,10},{9,11},{10,... | collective-permute-start | bytes 786440 | tf_op jit(solution)/shard_map/ppermute | solution.py:31
  96.5 10.5 %collective-permute-start.18 = (f32[2,128,256]{2,1,0:T(8,128)S(1)}, f32[2,128,256]{2,1,0:T(8,128)S(1)}, u32[]{:S(2)}, u32[]{:S(2)}) collective-permute-start(f32[2,128,256]{2,1,0:T(8,128)S(1)} %get-tuple-element.39), channel_id=1, source_target_pairs={{0,6},{1,7},{2,0},{3,1},{4,2},{5,3},{6,4},{7,5},{8,14},{9,15},{10,... | collective-permute-start | bytes 786440 | tf_op jit(solution)/shard_map/ppermute | solution.py:31
  98.1 10.8 %collective-permute-start.19 = (f32[2,128,256]{2,1,0:T(8,128)S(1)}, f32[2,128,256]{2,1,0:T(8,128)S(1)}, u32[]{:S(2)}, u32[]{:S(2)}) collective-permute-start(f32[2,128,256]{2,1,0:T(8,128)S(1)} %get-tuple-element.40), channel_id=1, source_target_pairs={{0,4},{1,5},{2,6},{3,7},{4,0},{5,1},{6,2},{7,3},{8,12},{9,13},{10,... | collective-permute-start | bytes 786440 | tf_op jit(solution)/shard_map/ppermute | solution.py:31
  100.2 20.9 %collective-permute-start.20 = (f32[4,128,256]{2,1,0:T(8,128)S(1)}, f32[4,128,256]{2,1,0:T(8,128)S(1)}, u32[]{:S(2)}, u32[]{:S(2)}) collective-permute-start(f32[4,128,256]{2,1,0:T(8,128)S(1)} %get-tuple-element.42), channel_id=1, source_target_pairs={{0,8},{1,9},{2,10},{3,11},{4,12},{5,13},{6,14},{7,15},{8,0},{9,1},... | collective-permute-start | bytes 1572872 | tf_op jit(solution)/shard_map/ppermute | solution.py:39
  101.6 22.5 %collective-permute-start.12 = (f32[4,128,256]{2,1,0:T(8,128)S(1)}, f32[4,128,256]{2,1,0:T(8,128)S(1)}, u32[]{:S(2)}, u32[]{:S(2)}) collective-permute-start(f32[4,128,256]{2,1,0:T(8,128)S(1)} %get-tuple-element.36), channel_id=1, source_target_pairs={{0,8},{1,9},{2,10},{3,11},{4,12},{5,13},{6,14},{7,15},{8,0},{9,1},... | collective-permute-start | bytes 1572872 | tf_op jit(solution)/shard_map/ppermute | solution.py:39
  107.0 8.9 %collective-permute-start.10 = (f32[2,128,256]{2,1,0:T(8,128)S(1)}, f32[2,128,256]{2,1,0:T(8,128)S(1)}, u32[]{:S(2)}, u32[]{:S(2)}) collective-permute-start(f32[2,128,256]{2,1,0:T(8,128)S(1)} %get-tuple-element.33), channel_id=1, source_target_pairs={{0,6},{1,7},{2,0},{3,1},{4,2},{5,3},{6,4},{7,5},{8,14},{9,15},{10,... | collective-permute-start | bytes 786440 | tf_op jit(solution)/shard_map/ppermute | solution.py:31
  107.0 8.9 %collective-permute-start.11 = (f32[2,128,256]{2,1,0:T(8,128)S(1)}, f32[2,128,256]{2,1,0:T(8,128)S(1)}, u32[]{:S(2)}, u32[]{:S(2)}) collective-permute-start(f32[2,128,256]{2,1,0:T(8,128)S(1)} %get-tuple-element.34), channel_id=1, source_target_pairs={{0,4},{1,5},{2,6},{3,7},{4,0},{5,1},{6,2},{7,3},{8,12},{9,13},{10,... | collective-permute-start | bytes 786440 | tf_op jit(solution)/shard_map/ppermute | solution.py:31
  109.0 12.1 %collective-permute-start.9 = (f32[2,128,256]{2,1,0:T(8,128)S(1)}, f32[2,128,256]{2,1,0:T(8,128)S(1)}, u32[]{:S(2)}, u32[]{:S(2)}) collective-permute-start(f32[2,128,256]{2,1,0:T(8,128)S(1)} %get-tuple-element.32), channel_id=1, source_target_pairs={{0,2},{1,3},{2,4},{3,5},{4,6},{5,7},{6,0},{7,1},{8,10},{9,11},{10,... | collective-permute-start | bytes 786440 | tf_op jit(solution)/shard_map/ppermute | solution.py:31
  127.2 27.7 %all-to-all-start.2 = ((f32[64,8,512]{2,1,0:T(8,128)}), f32[64,8,512]{2,1,0:T(8,128)S(1)}, u32[]{:S(2)}, u32[]{:S(2)}) async-start(f32[64,8,512]{2,1,0:T(8,128)} %bitcast.25), calls=%async_computation.2 | async-start | bytes 2097152 | tf_op jit(solution)/shard_map/all_to_all | solution.py:245
  156.8 21.8 %all-to-all-start.3 = ((f32[64,8,512]{2,1,0:T(8,128)}), f32[64,8,512]{2,1,0:T(8,128)S(1)}, u32[]{:S(2)}, u32[]{:S(2)}) async-start(f32[64,8,512]{2,1,0:T(8,128)} %broadcast_in_dim.9), calls=%async_computation.3 | async-start | bytes 2097152 | tf_op jit(solution)/shard_map/all_to_all | solution.py:249
  162.0 22.1 %collective-permute-start.26 = (f32[2,128,256]{2,1,0:T(8,128)S(1)}, f32[2,128,256]{2,1,0:T(8,128)S(1)}, u32[]{:S(2)}, u32[]{:S(2)}) collective-permute-start(f32[2,128,256]{2,1,0:T(8,128)S(1)} %get-tuple-element.44), channel_id=1, source_target_pairs={{0,8},{1,9},{2,10},{3,11},{4,12},{5,13},{6,14},{7,15},{8,0},{9,1},... | collective-permute-start | bytes 786440 | tf_op jit(solution)/shard_map/ppermute | solution.py:39
  163.1 21.0 %collective-permute-start.27 = (f32[2,128,256]{2,1,0:T(8,128)S(1)}, f32[2,128,256]{2,1,0:T(8,128)S(1)}, u32[]{:S(2)}, u32[]{:S(2)}) collective-permute-start(f32[2,128,256]{2,1,0:T(8,128)S(1)} %get-tuple-element.46), channel_id=1, source_target_pairs={{0,2},{1,3},{2,4},{3,5},{4,6},{5,7},{6,0},{7,1},{8,10},{9,11},{10,... | collective-permute-start | bytes 786440 | tf_op jit(solution)/shard_map/ppermute | solution.py:31
  164.3 19.8 %collective-permute-start.28 = (f32[2,128,256]{2,1,0:T(8,128)S(1)}, f32[2,128,256]{2,1,0:T(8,128)S(1)}, u32[]{:S(2)}, u32[]{:S(2)}) collective-permute-start(f32[2,128,256]{2,1,0:T(8,128)S(1)} %get-tuple-element.47), channel_id=1, source_target_pairs={{0,6},{1,7},{2,0},{3,1},{4,2},{5,3},{6,4},{7,5},{8,14},{9,15},{10,... | collective-permute-start | bytes 786440 | tf_op jit(solution)/shard_map/ppermute | solution.py:31
  165.8 20.0 %collective-permute-start.29 = (f32[2,128,256]{2,1,0:T(8,128)S(1)}, f32[2,128,256]{2,1,0:T(8,128)}, u32[]{:S(2)}, u32[]{:S(2)}) collective-permute-start(f32[2,128,256]{2,1,0:T(8,128)S(1)} %get-tuple-element.48), channel_id=1, source_target_pairs={{0,4},{1,5},{2,6},{3,7},{4,0},{5,1},{6,2},{7,3},{8,12},{9,13},{10,... | collective-permute-start | bytes 786440 | tf_op jit(solution)/shard_map/ppermute | solution.py:31
  178.6 13.3 %collective-permute-start.31 = (f32[512,512]{1,0:T(8,128)S(1)}, f32[512,512]{1,0:T(8,128)S(1)}, u32[]{:S(2)}, u32[]{:S(2)}) collective-permute-start(f32[512,512]{1,0:T(8,128)S(1)} %bitcast.43), channel_id=1, source_target_pairs={{0,1},{1,0},{2,3},{3,2},{4,5},{5,4},{6,7},{7,6},{8,9},{9,8},{10,11... | collective-permute-start | bytes 3145736 | tf_op jit(solution)/shard_map/ppermute | solution.py:27
  (6 other events, 103.1 us)

commit v3 on v2

--- a/solution.py
+++ b/solution.py
@@ -213,18 +213,15 @@
 
     spread = lax.all_to_all(factor.reshape(2, 8, 16, WIDTH), ROW, 1, 0)
     spread = lax.all_to_all(spread.reshape(16, 16, WIDTH), COL, 0, 0)
-    low, high = spread[:8], spread[8:]
-    low_y, *high_z = lax.optimization_barrier(
-        (to_y(low, 2), high, *(to_z(high, s) for s in (1, 2, 3)))
-    )
-    pair = jnp.stack([low, low_y])
-    quad = jnp.stack(high_z)
-
     gathered = []
     for c in range(2):
-        cut = lambda v: v[..., c * half : (c + 1) * half]
-        pairs = [cut(pair)] + [to_z(cut(pair), s) for s in (1, 2, 3)]
-        gathered.append([*pairs, cut(quad), to_y(cut(quad), 2)])
+        low, high = (v[:, :, c * half : (c + 1) * half] for v in (spread[:8], spread[8:]))
+        low_y, *high_z = lax.optimization_barrier(
+            (to_y(low, 2), high, *(to_z(high, s) for s in (1, 2, 3)))
+        )
+        pair, quad = jnp.stack([low, low_y]), jnp.stack(high_z)
+        pairs = [pair] + [to_z(pair, s) for s in (1, 2, 3)]
+        gathered.append([*pairs, quad, to_y(quad, 2)])
 
     parts = []
     for c in range(2):

time: 194 us -> 196 us (1.010)
  waiting for transfers between devices: 72.6 us -> 78.9 us
  other arithmetic: 6.82 us -> 4.86 us
    ppermute x4, starting transfers between devices: 16.9 us -> 10 us  [to_core(): return lax.ppermute(v, AXES, route(lambda z, y, x, c: (z, y, x, 1 - c)))]
    ppermute x12, starting transfers between devices: 15.1 us -> 20.8 us  [to_x(): return lax.ppermute(v, AXES, route(lambda z, y, x, c: (z, y, x + s, c)))]
    ppermute x12, waiting for transfers between devices: 17.3 us -> 22.1 us  [to_x(): return lax.ppermute(v, AXES, route(lambda z, y, x, c: (z, y, x + s, c)))]
    ppermute x3 -> x4, waiting for transfers between devices: 0.01 us -> 2.9 us  [to_y(): return lax.ppermute(v, AXES, route(lambda z, y, x, c: (z, y + s, x, c)))]
    ppermute x4, waiting for transfers between devices: 3.09 us -> 1.01 us  [to_yl(): return lax.ppermute(v, AXES, route(lambda z, y, x, c: (z, y ^ 1, x, c)))]
    ppermute x3 -> x4, starting transfers between devices: 4.14 us -> 5.43 us  [to_y(): return lax.ppermute(v, AXES, route(lambda z, y, x, c: (z, y + s, x, c)))]
    ppermute x9 -> x12, waiting for transfers between devices: 12.8 us -> 13.8 us  [to_z(): return lax.ppermute(v, AXES, route(lambda z, y, x, c: (z + s, y, x, c)))]
    ppermute x9 -> x12, starting transfers between devices: 9.69 us -> 9.53 us  [to_z(): return lax.ppermute(v, AXES, route(lambda z, y, x, c: (z + s, y, x, c)))]
  transfers between devices with their start and end apart: 35 -> 39, of which waited for: 14 -> 18; matrix products, arithmetic and copies ran while one was open for 3% -> 2% of each run, Pallas kernels for 9% -> 9%
where the time goes in v3:
time: 196 us
  waiting for transfers between devices  78.9 us (40%)
  starting transfers between devices  69.6 us (36%)
  Pallas kernels  19.7 us (10%)
  blocking collectives  19 us (10%)
  other arithmetic  4.86 us (2%)
  local copies, waits for them, and re-layouts  2.69 us (1%)
    ppermute x12, waiting for transfers between devices, to_x(): return lax.ppermute(v, AXES, route(lambda z, y, x, c: (z, y, x + s, c)))  22.1 us
    ppermute x12, starting transfers between devices, to_x(): return lax.ppermute(v, AXES, route(lambda z, y, x, c: (z, y, x + s, c)))  20.8 us
    all_to_all x1, blocking collectives, per_device(): spread = lax.all_to_all(factor.reshape(2, 8, 16, WIDTH), ROW, 1, 0)  19 us
    all_to_all x1, waiting for transfers between devices, per_device(): diag = lax.all_to_all(diag.reshape(64, 8, WIDTH), CHIPS, 0, 0)  17.4 us
    pallas_call x2, Pallas kernels, panel(): pl.pallas_call(panel_kernel, grid_spec=pltpu.PrefetchScalarGridSpec(num_s...  16.7 us
    ppermute x12, waiting for transfers between devices, to_z(): return lax.ppermute(v, AXES, route(lambda z, y, x, c: (z + s, y, x, c)))  13.8 us
    all_to_all x1, waiting for transfers between devices, per_device(): diag = lax.all_to_all(jnp.broadcast_to(diag, (64, 8, WIDTH)), CHIPS, 0, 0)  11.4 us
    ppermute x4, starting transfers between devices, to_core(): return lax.ppermute(v, AXES, route(lambda z, y, x, c: (z, y, x, 1 - c)))  10 us
  transfers between devices with their start and end apart: 39, of which 18 were waited for; matrix products, arithmetic and copies ran while one was open for 2% of the time, Pallas kernels for 9%

profile of v3, /device:TPU:1, one launch (start us, length us, event | category | flops | bytes accessed | tf_op | source)
XLA Modules:
  0.0 195.7 jit_solution(16198262560873555661)
XLA Ops:
  0.7 1.5 collective-permute-start
  3.2 19.0 %all_to_all.30 = f32[1,2,8,16,512]{4,3,1,0,2:T(8,128)} all-to-all(f32[1,2,8,16,512]{4,3,1,0,2:T(8,128)S(1)} %copy.17), channel_id=1, replica_groups=mesh['z'=4,'yh'=2,'yl'=2,'x'=4,'core'=2] {'z','yh'}, dimensions={2} | all-to-all | bytes 1048576 | tf_op jit(solution)/shard_map/all_to_all | solution.py:214
  22.2 5.6 %all-to-all-start.1 = ((f32[16,16,512]{2,1,0:T(8,128)}), f32[16,16,512]{2,1,0:T(8,128)S(1)}, u32[]{:S(2)}, u32[]{:S(2)}) async-start(f32[16,16,512]{2,1,0:T(8,128)} %bitcast.9), calls=%async_computation.1 | async-start | bytes 1048576 | tf_op jit(solution)/shard_map/all_to_all | solution.py:215
  28.2 9.1 %all-to-all-done.1 = f32[16,16,512]{2,1,0:T(8,128)S(1)} async-done(((f32[16,16,512]{2,1,0:T(8,128)}), f32[16,16,512]{2,1,0:T(8,128)S(1)}, u32[]{:S(2)}, u32[]{:S(2)}) %all-to-all-start.1) | async-done | bytes 524320 | tf_op jit(solution)/shard_map/all_to_all | solution.py:215
  37.5 1.7 collective-permute-start.15
  40.5 4.2 %collective-permute-done.14 = f32[8,16,256]{2,1,0:T(8,128)S(1)} collective-permute-done((f32[8,16,256]{2,1,0:T(8,128)S(1)}, f32[8,16,256]{2,1,0:T(8,128)S(1)}, u32[]{:S(2)}, u32[]{:S(2)}) %collective-permute-start.14) | collective-permute-done | bytes 131104 | tf_op jit(solution)/shard_map/ppermute | solution.py:43
  47.2 2.8 %collective-permute-done.13 = f32[8,16,256]{2,1,0:T(8,128)S(1)} collective-permute-done((f32[8,16,256]{2,1,0:T(8,128)S(1)}, f32[8,16,256]{2,1,0:T(8,128)S(1)}, u32[]{:S(2)}, u32[]{:S(2)}) %collective-permute-start.13) | collective-permute-done | bytes 131104 | tf_op jit(solution)/shard_map/ppermute | solution.py:35
  51.2 1.5 collective-permute-done.2
  52.7 1.6 collective-permute-start.20
  55.7 1.5 collective-permute-start.19
  57.3 7.3 %collective-permute-done.17.rest_1_ = f32[2,8,16,256]{3,2,1,0:T(8,128)S(1)} collective-permute-done((f32[2,8,16,256]{3,2,1,0:T(8,128)S(1)}, f32[2,8,16,256]{3,2,1,0:T(8,128)S(1)}, u32[]{:S(2)}, u32[]{:S(2)}) %collective-permute-start.17) | collective-permute-done | bytes 262176 | tf_op jit(solution)/shard_map/ppermute | solution.py:43
  64.6 9.6 %collective-permute-start.27 = (f32[512,128]{1,0:T(8,128)S(1)}, f32[512,128]{1,0:T(8,128)S(1)}, u32[]{:S(2)}, u32[]{:S(2)}) collective-permute-start(f32[512,128]{1,0:T(8,128)S(1)} %get-tuple-element.66.refs_14_), channel_id=1, source_target_pairs={{0,6},{1,7},{2,0},{3,1},{4,2},{5,3},{6,4},{7,5},{8,14},{9,15},{10,... | collective-permute-start | bytes 786440 | tf_op jit(solution)/shard_map/ppermute | solution.py:31
  74.5 2.4 %collective-permute-start.7 = (f32[2,8,16,256]{3,2,1,0:T(8,128)S(1)}, f32[2,8,16,256]{3,2,1,0:T(8,128)S(1)}, u32[]{:S(2)}, u32[]{:S(2)}) collective-permute-start(f32[2,8,16,256]{3,2,1,0:T(8,128)S(1)} %pad_maximum_fusion.3.rest_0_), channel_id=1, source_target_pairs={{0,96},{1,97},{2,98},{3,99},{4,100},{5,101},{6,102},{7,103},{8,104... | collective-permute-start | bytes 786440 | tf_op jit(solution)/shard_map/ppermute | solution.py:43
  76.9 1.7 collective-permute-start.8
  78.6 8.3 %shard_map.60 = (f32[2,128,256]{2,1,0:T(8,128)S(1)}, f32[2,128,256]{2,1,0:T(8,128)S(1)}, f32[2,128,256]{2,1,0:T(8,128)S(1)}, f32[2,128,256]{2,1,0:T(8,128)S(1)},...) custom-call(s32[17]{0:T(128)S(1)} %concatenate.6.info, f32[2048,1024]{1,0:T(8,128)} %own.3, ...), custom_call_target="tpu_custom_call" | custom-call | flops 6442450944 | bytes 20971520 | tf_op jit(solution)/shard_map/pallas_call | solution.py:123
  90.7 8.3 %shard_map.59 = (f32[2,128,256]{2,1,0:T(8,128)S(1)}, f32[2,128,256]{2,1,0:T(8,128)S(1)}, f32[2,128,256]{2,1,0:T(8,128)S(1)}, f32[2,128,256]{2,1,0:T(8,128)S(1)},...) custom-call(s32[17]{0:T(128)S(1)} %concatenate.6.info, f32[2048,1024]{1,0:T(8,128)} %own.3, ...), custom_call_target="tpu_custom_call" | custom-call | flops 6442450944 | bytes 20971520 | tf_op jit(solution)/shard_map/pallas_call | solution.py:123
  99.8 2.5 %collective-permute-start.23 = (f32[2,128,256]{2,1,0:T(8,128)S(1)}, f32[2,128,256]{2,1,0:T(8,128)S(1)}, u32[]{:S(2)}, u32[]{:S(2)}) collective-permute-start(f32[2,128,256]{2,1,0:T(8,128)S(1)} %get-tuple-element.50), channel_id=1, source_target_pairs={{0,4},{1,5},{2,6},{3,7},{4,0},{5,1},{6,2},{7,3},{8,12},{9,13},{10,... | collective-permute-start | bytes 786440 | tf_op jit(solution)/shard_map/ppermute | solution.py:31
  104.5 6.3 %collective-permute-done.21.refs_7_ = f32[2,128,256]{2,1,0:T(8,128)S(1)} collective-permute-done((f32[2,128,256]{2,1,0:T(8,128)S(1)}, f32[2,128,256]{2,1,0:T(8,128)S(1)}, u32[]{:S(2)}, u32[]{:S(2)}) %collective-permute-start.21) | collective-permute-done | bytes 262176 | tf_op jit(solution)/shard_map/ppermute | solution.py:31
  112.1 1.8 collective-permute-start.9
  114.0 4.1 %collective-permute-done.10.refs_2_ = f32[2,128,256]{2,1,0:T(8,128)S(1)} collective-permute-done((f32[2,128,256]{2,1,0:T(8,128)S(1)}, f32[2,128,256]{2,1,0:T(8,128)S(1)}, u32[]{:S(2)}, u32[]{:S(2)}) %collective-permute-start.10) | collective-permute-done | bytes 262176 | tf_op jit(solution)/shard_map/ppermute | solution.py:31
  118.9 7.2 %collective-permute-done.9.refs_1_ = f32[2,128,256]{2,1,0:T(8,128)S(1)} collective-permute-done((f32[2,128,256]{2,1,0:T(8,128)S(1)}, f32[2,128,256]{2,1,0:T(8,128)S(1)}, u32[]{:S(2)}, u32[]{:S(2)}) %collective-permute-start.9) | collective-permute-done | bytes 262176 | tf_op jit(solution)/shard_map/ppermute | solution.py:31
  127.1 3.1 %shard_map.61 = (f32[512,512]{1,0:T(8,128)}, f32[2,128,256]{2,1,0:T(8,128)S(1)}, f32[2,128,256]{2,1,0:T(8,128)S(1)}, f32[2,128,256]{2,1,0:T(8,128)S(1)}, f32[2,1...) custom-call(s32[17]{0:T(128)S(1)} %concatenate.6.info, ...), custom_call_target="tpu_custom_call" | custom-call | flops 1207959552 | bytes 9437184 | tf_op jit(solution)/shard_map/pallas_call | solution.py:169
  130.1 9.6 %all-to-all-start.2 = ((f32[64,8,512]{2,1,0:T(8,128)}), f32[64,8,512]{2,1,0:T(8,128)S(1)}, u32[]{:S(2)}, u32[]{:S(2)}) async-start(f32[64,8,512]{2,1,0:T(8,128)} %bitcast.31), calls=%async_computation.2 | async-start | bytes 2097152 | tf_op jit(solution)/shard_map/all_to_all | solution.py:242
  139.7 17.4 %all-to-all-done.2 = f32[64,8,512]{2,1,0:T(8,128)S(1)} async-done(((f32[64,8,512]{2,1,0:T(8,128)}), f32[64,8,512]{2,1,0:T(8,128)S(1)}, u32[]{:S(2)}, u32[]{:S(2)}) %all-to-all-start.2) | async-done | bytes 1048608 | tf_op jit(solution)/shard_map/all_to_all | solution.py:242
  159.0 5.2 %all-to-all-start.3 = ((f32[64,8,512]{2,1,0:T(8,128)}), f32[64,8,512]{2,1,0:T(8,128)S(1)}, u32[]{:S(2)}, u32[]{:S(2)}) async-start(f32[64,8,512]{2,1,0:T(8,128)} %broadcast_in_dim.9), calls=%async_computation.3 | async-start | bytes 2097152 | tf_op jit(solution)/shard_map/all_to_all | solution.py:246
  166.5 1.5 collective-permute-start.32
  168.0 1.5 collective-permute-start.33
  169.5 11.4 %all-to-all-done.3 = f32[64,8,512]{2,1,0:T(8,128)S(1)} async-done(((f32[64,8,512]{2,1,0:T(8,128)}), f32[64,8,512]{2,1,0:T(8,128)S(1)}, u32[]{:S(2)}, u32[]{:S(2)}) %all-to-all-start.3) | async-done | bytes 1048608 | tf_op jit(solution)/shard_map/all_to_all | solution.py:246
  180.8 5.5 %collective-permute-start.35 = (f32[512,512]{1,0:T(8,128)S(1)}, f32[512,512]{1,0:T(8,128)S(1)}, u32[]{:S(2)}, u32[]{:S(2)}) collective-permute-start(f32[512,512]{1,0:T(8,128)S(1)} %bitcast.50), channel_id=1, source_target_pairs={{0,1},{1,0},{2,3},{3,2},{4,5},{5,4},{6,7},{7,6},{8,9},{9,8},{10,11... | collective-permute-start | bytes 3145736 | tf_op jit(solution)/shard_map/ppermute | solution.py:27
  186.3 1.7 collective-permute-done.33
  189.1 2.9 %collective-permute-start.34 = (f32[2,128,256]{2,1,0:T(8,128)S(1)}, f32[2,128,256]{2,1,0:T(8,128)S(1)}, u32[]{:S(2)}, u32[]{:S(2)}) collective-permute-start(f32[2,128,256]{2,1,0:T(8,128)S(1)} %broadcast_select_fusion), channel_id=1, source_target_pairs={{0,1},{1,0},{2,3},{3,2},{4,5},{5,4},{6,7},{7,6},{8,9},{9,8},{10,11... | collective-permute-start | bytes 786440 | tf_op jit(solution)/shard_map/ppermute | solution.py:27
  194.1 1.6 maximum_select_fusion
  (80 shorter events, 25.6 us)
Async XLA Ops:
  0.7 76.3 %collective-permute-start = (f32[2048,1024]{1,0:T(8,128)}, f32[2048,1024]{1,0:T(8,128)}, u32[]{:S(2)}, u32[]{:S(2)}) collective-permute-start(f32[2048,1024]{1,0:T(8,128)} %own.3), channel_id=1, source_target_pairs={{0,1},{1,0},{2,3},{3,2},{4,5},{5,4},{6,7},{7,6},{8,9},{9,8},{10,11... | collective-permute-start | bytes 25165832 | tf_op jit(solution)/shard_map/ppermute | solution.py:27
  22.2 15.1 %all-to-all-start.1 = ((f32[16,16,512]{2,1,0:T(8,128)}), f32[16,16,512]{2,1,0:T(8,128)S(1)}, u32[]{:S(2)}, u32[]{:S(2)}) async-start(f32[16,16,512]{2,1,0:T(8,128)} %bitcast.9), calls=%async_computation.1 | async-start | bytes 1048576 | tf_op jit(solution)/shard_map/all_to_all | solution.py:215
  28.0 22.0 %collective-permute-start.25 = (f32[512,128]{1,0:T(8,128)S(1)}, f32[512,128]{1,0:T(8,128)S(1)}, u32[]{:S(2)}, u32[]{:S(2)}) collective-permute-start(f32[512,128]{1,0:T(8,128)S(1)} %bitcast.56), channel_id=1, source_target_pairs={{0,1},{1,0},{2,3},{3,2},{4,5},{5,4},{6,7},{7,6},{8,9},{9,8},{10,11... | collective-permute-start | bytes 786440 | tf_op jit(solution)/shard_map/ppermute | solution.py:27
  37.4 7.3 %collective-permute-start.14 = (f32[8,16,256]{2,1,0:T(8,128)S(1)}, f32[8,16,256]{2,1,0:T(8,128)S(1)}, u32[]{:S(2)}, u32[]{:S(2)}) collective-permute-start(f32[8,16,256]{2,1,0:T(8,128)S(1)} %get-tuple-element.43), channel_id=1, source_target_pairs={{0,32},{1,33},{2,34},{3,35},{4,36},{5,37},{6,38},{7,39},{8,40},{9,... | collective-permute-start | bytes 393224 | tf_op jit(solution)/shard_map/ppermute | solution.py:43
  37.5 8.4 %collective-permute-start.15 = (f32[8,16,256]{2,1,0:T(8,128)S(1)}, f32[8,16,256]{2,1,0:T(8,128)S(1)}, u32[]{:S(2)}, u32[]{:S(2)}) collective-permute-start(f32[8,16,256]{2,1,0:T(8,128)S(1)} %get-tuple-element.43), channel_id=1, source_target_pairs={{0,64},{1,65},{2,66},{3,67},{4,68},{5,69},{6,70},{7,71},{8,72},{9,... | collective-permute-start | bytes 393224 | tf_op jit(solution)/shard_map/ppermute | solution.py:43
  46.4 8.0 %collective-permute-start.3 = (f32[8,16,256]{2,1,0:T(8,128)S(1)}, f32[8,16,256]{2,1,0:T(8,128)S(1)}, u32[]{:S(2)}, u32[]{:S(2)}) collective-permute-start(f32[8,16,256]{2,1,0:T(8,128)S(1)} %get-tuple-element.32), channel_id=1, source_target_pairs={{0,64},{1,65},{2,66},{3,67},{4,68},{5,69},{6,70},{7,71},{8,72},{9,... | collective-permute-start | bytes 393224 | tf_op jit(solution)/shard_map/ppermute | solution.py:43
  52.7 21.8 %collective-permute-start.20 = (f32[4,8,16,256]{3,2,1,0:T(8,128)S(1)}, f32[4,8,16,256]{3,2,1,0:T(8,128)S(1)}, u32[]{:S(2)}, u32[]{:S(2)}) collective-permute-start(f32[4,8,16,256]{3,2,1,0:T(8,128)S(1)} %pad_maximum_fusion.1.rest_4_), channel_id=1, source_target_pairs={{0,16},{1,17},{2,18},{3,19},{4,20},{5,21},{6,22},{7,23},{8,24},{9,... | collective-permute-start | bytes 1572872 | tf_op jit(solution)/shard_map/ppermute | solution.py:35
  54.3 10.2 %collective-permute-start.17 = (f32[2,8,16,256]{3,2,1,0:T(8,128)S(1)}, f32[2,8,16,256]{3,2,1,0:T(8,128)S(1)}, u32[]{:S(2)}, u32[]{:S(2)}) collective-permute-start(f32[2,8,16,256]{3,2,1,0:T(8,128)S(1)} %pad_maximum_fusion.4.rest_0_), channel_id=1, source_target_pairs={{0,32},{1,33},{2,34},{3,35},{4,36},{5,37},{6,38},{7,39},{8,40},{9,... | collective-permute-start | bytes 786440 | tf_op jit(solution)/shard_map/ppermute | solution.py:43
  54.7 19.5 %collective-permute-start.18 = (f32[2,8,16,256]{3,2,1,0:T(8,128)S(1)}, f32[2,8,16,256]{3,2,1,0:T(8,128)S(1)}, u32[]{:S(2)}, u32[]{:S(2)}) collective-permute-start(f32[2,8,16,256]{3,2,1,0:T(8,128)S(1)} %pad_maximum_fusion.4.rest_0_), channel_id=1, source_target_pairs={{0,64},{1,65},{2,66},{3,67},{4,68},{5,69},{6,70},{7,71},{8,72},{9,... | collective-permute-start | bytes 786440 | tf_op jit(solution)/shard_map/ppermute | solution.py:43
  55.7 18.5 %collective-permute-start.19 = (f32[2,8,16,256]{3,2,1,0:T(8,128)S(1)}, f32[2,8,16,256]{3,2,1,0:T(8,128)S(1)}, u32[]{:S(2)}, u32[]{:S(2)}) collective-permute-start(f32[2,8,16,256]{3,2,1,0:T(8,128)S(1)} %pad_maximum_fusion.4.rest_0_), channel_id=1, source_target_pairs={{0,96},{1,97},{2,98},{3,99},{4,100},{5,101},{6,102},{7,103},{8,104... | collective-permute-start | bytes 786440 | tf_op jit(solution)/shard_map/ppermute | solution.py:43
  64.6 34.5 %collective-permute-start.27 = (f32[512,128]{1,0:T(8,128)S(1)}, f32[512,128]{1,0:T(8,128)S(1)}, u32[]{:S(2)}, u32[]{:S(2)}) collective-permute-start(f32[512,128]{1,0:T(8,128)S(1)} %get-tuple-element.66.refs_14_), channel_id=1, source_target_pairs={{0,6},{1,7},{2,0},{3,1},{4,2},{5,3},{6,4},{7,5},{8,14},{9,15},{10,... | collective-permute-start | bytes 786440 | tf_op jit(solution)/shard_map/ppermute | solution.py:31
  74.2 13.6 %collective-permute-start.5 = (f32[2,8,16,256]{3,2,1,0:T(8,128)S(1)}, f32[2,8,16,256]{3,2,1,0:T(8,128)S(1)}, u32[]{:S(2)}, u32[]{:S(2)}) collective-permute-start(f32[2,8,16,256]{3,2,1,0:T(8,128)S(1)} %pad_maximum_fusion.3.rest_0_), channel_id=1, source_target_pairs={{0,32},{1,33},{2,34},{3,35},{4,36},{5,37},{6,38},{7,39},{8,40},{9,... | collective-permute-start | bytes 786440 | tf_op jit(solution)/shard_map/ppermute | solution.py:43
  74.2 13.9 %collective-permute-start.6 = (f32[2,8,16,256]{3,2,1,0:T(8,128)S(1)}, f32[2,8,16,256]{3,2,1,0:T(8,128)S(1)}, u32[]{:S(2)}, u32[]{:S(2)}) collective-permute-start(f32[2,8,16,256]{3,2,1,0:T(8,128)S(1)} %pad_maximum_fusion.3.rest_0_), channel_id=1, source_target_pairs={{0,64},{1,65},{2,66},{3,67},{4,68},{5,69},{6,70},{7,71},{8,72},{9,... | collective-permute-start | bytes 786440 | tf_op jit(solution)/shard_map/ppermute | solution.py:43
  74.5 13.9 %collective-permute-start.7 = (f32[2,8,16,256]{3,2,1,0:T(8,128)S(1)}, f32[2,8,16,256]{3,2,1,0:T(8,128)S(1)}, u32[]{:S(2)}, u32[]{:S(2)}) collective-permute-start(f32[2,8,16,256]{3,2,1,0:T(8,128)S(1)} %pad_maximum_fusion.3.rest_0_), channel_id=1, source_target_pairs={{0,96},{1,97},{2,98},{3,99},{4,100},{5,101},{6,102},{7,103},{8,104... | collective-permute-start | bytes 786440 | tf_op jit(solution)/shard_map/ppermute | solution.py:43
  76.9 12.4 %collective-permute-start.8 = (f32[4,8,16,256]{3,2,1,0:T(8,128)S(1)}, f32[4,8,16,256]{3,2,1,0:T(8,128)S(1)}, u32[]{:S(2)}, u32[]{:S(2)}) collective-permute-start(f32[4,8,16,256]{3,2,1,0:T(8,128)S(1)} %pad_maximum_fusion.rest_4_), channel_id=1, source_target_pairs={{0,16},{1,17},{2,18},{3,19},{4,20},{5,21},{6,22},{7,23},{8,24},{9,... | collective-permute-start | bytes 1572872 | tf_op jit(solution)/shard_map/ppermute | solution.py:35
  87.8 12.0 %collective-permute-start.28 = (f32[512,128]{1,0:T(8,128)S(1)}, f32[512,128]{1,0:T(8,128)S(1)}, u32[]{:S(2)}, u32[]{:S(2)}) collective-permute-start(f32[512,128]{1,0:T(8,128)S(1)} %get-tuple-element.66.refs_14_), channel_id=1, source_target_pairs={{0,4},{1,5},{2,6},{3,7},{4,0},{5,1},{6,2},{7,3},{8,12},{9,13},{10,... | collective-permute-start | bytes 786440 | tf_op jit(solution)/shard_map/ppermute | solution.py:31
  88.0 15.0 %collective-permute-start.29 = (f32[512,128]{1,0:T(8,128)S(1)}, f32[512,128]{1,0:T(8,128)S(1)}, u32[]{:S(2)}, u32[]{:S(2)}) collective-permute-start(f32[512,128]{1,0:T(8,128)S(1)} %get-tuple-element.66.refs_14_), channel_id=1, source_target_pairs={{0,2},{1,3},{2,4},{3,5},{4,6},{5,7},{6,0},{7,1},{8,10},{9,11},{10,... | collective-permute-start | bytes 786440 | tf_op jit(solution)/shard_map/ppermute | solution.py:31
  88.4 15.3 %collective-permute-start.26 = (f32[512,128]{1,0:T(8,128)S(1)}, f32[512,128]{1,0:T(8,128)S(1)}, u32[]{:S(2)}, u32[]{:S(2)}) collective-permute-start(f32[512,128]{1,0:T(8,128)S(1)} %get-tuple-element.67.refs_12_), channel_id=1, source_target_pairs={{0,8},{1,9},{2,10},{3,11},{4,12},{5,13},{6,14},{7,15},{8,0},{9,1},... | collective-permute-start | bytes 786440 | tf_op jit(solution)/shard_map/ppermute | solution.py:39
  89.3 21.5 %collective-permute-start.21 = (f32[2,128,256]{2,1,0:T(8,128)S(1)}, f32[2,128,256]{2,1,0:T(8,128)S(1)}, u32[]{:S(2)}, u32[]{:S(2)}) collective-permute-start(f32[2,128,256]{2,1,0:T(8,128)S(1)} %get-tuple-element.48), channel_id=1, source_target_pairs={{0,2},{1,3},{2,4},{3,5},{4,6},{5,7},{6,0},{7,1},{8,10},{9,11},{10,... | collective-permute-start | bytes 786440 | tf_op jit(solution)/shard_map/ppermute | solution.py:31
  99.0 11.8 %collective-permute-start.22 = (f32[2,128,256]{2,1,0:T(8,128)S(1)}, f32[2,128,256]{2,1,0:T(8,128)S(1)}, u32[]{:S(2)}, u32[]{:S(2)}) collective-permute-start(f32[2,128,256]{2,1,0:T(8,128)S(1)} %get-tuple-element.49), channel_id=1, source_target_pairs={{0,6},{1,7},{2,0},{3,1},{4,2},{5,3},{6,4},{7,5},{8,14},{9,15},{10,... | collective-permute-start | bytes 786440 | tf_op jit(solution)/shard_map/ppermute | solution.py:31
  99.8 12.4 %collective-permute-start.23 = (f32[2,128,256]{2,1,0:T(8,128)S(1)}, f32[2,128,256]{2,1,0:T(8,128)S(1)}, u32[]{:S(2)}, u32[]{:S(2)}) collective-permute-start(f32[2,128,256]{2,1,0:T(8,128)S(1)} %get-tuple-element.50), channel_id=1, source_target_pairs={{0,4},{1,5},{2,6},{3,7},{4,0},{5,1},{6,2},{7,3},{8,12},{9,13},{10,... | collective-permute-start | bytes 786440 | tf_op jit(solution)/shard_map/ppermute | solution.py:31
  103.1 23.0 %collective-permute-start.24 = (f32[4,128,256]{2,1,0:T(8,128)S(1)}, f32[4,128,256]{2,1,0:T(8,128)S(1)}, u32[]{:S(2)}, u32[]{:S(2)}) collective-permute-start(f32[4,128,256]{2,1,0:T(8,128)S(1)} %get-tuple-element.52), channel_id=1, source_target_pairs={{0,8},{1,9},{2,10},{3,11},{4,12},{5,13},{6,14},{7,15},{8,0},{9,1},... | collective-permute-start | bytes 1572872 | tf_op jit(solution)/shard_map/ppermute | solution.py:39
  103.7 23.4 %collective-permute-start.12 = (f32[4,128,256]{2,1,0:T(8,128)S(1)}, f32[4,128,256]{2,1,0:T(8,128)S(1)}, u32[]{:S(2)}, u32[]{:S(2)}) collective-permute-start(f32[4,128,256]{2,1,0:T(8,128)S(1)} %get-tuple-element.41), channel_id=1, source_target_pairs={{0,8},{1,9},{2,10},{3,11},{4,12},{5,13},{6,14},{7,15},{8,0},{9,1},... | collective-permute-start | bytes 1572872 | tf_op jit(solution)/shard_map/ppermute | solution.py:39
  110.8 8.0 %collective-permute-start.11 = (f32[2,128,256]{2,1,0:T(8,128)S(1)}, f32[2,128,256]{2,1,0:T(8,128)S(1)}, u32[]{:S(2)}, u32[]{:S(2)}) collective-permute-start(f32[2,128,256]{2,1,0:T(8,128)S(1)} %get-tuple-element.39), channel_id=1, source_target_pairs={{0,4},{1,5},{2,6},{3,7},{4,0},{5,1},{6,2},{7,3},{8,12},{9,13},{10,... | collective-permute-start | bytes 786440 | tf_op jit(solution)/shard_map/ppermute | solution.py:31
  112.1 13.9 %collective-permute-start.9 = (f32[2,128,256]{2,1,0:T(8,128)S(1)}, f32[2,128,256]{2,1,0:T(8,128)S(1)}, u32[]{:S(2)}, u32[]{:S(2)}) collective-permute-start(f32[2,128,256]{2,1,0:T(8,128)S(1)} %get-tuple-element.37), channel_id=1, source_target_pairs={{0,2},{1,3},{2,4},{3,5},{4,6},{5,7},{6,0},{7,1},{8,10},{9,11},{10,... | collective-permute-start | bytes 786440 | tf_op jit(solution)/shard_map/ppermute | solution.py:31
  130.1 27.0 %all-to-all-start.2 = ((f32[64,8,512]{2,1,0:T(8,128)}), f32[64,8,512]{2,1,0:T(8,128)S(1)}, u32[]{:S(2)}, u32[]{:S(2)}) async-start(f32[64,8,512]{2,1,0:T(8,128)} %bitcast.31), calls=%async_computation.2 | async-start | bytes 2097152 | tf_op jit(solution)/shard_map/all_to_all | solution.py:242
  159.0 21.8 %all-to-all-start.3 = ((f32[64,8,512]{2,1,0:T(8,128)}), f32[64,8,512]{2,1,0:T(8,128)S(1)}, u32[]{:S(2)}, u32[]{:S(2)}) async-start(f32[64,8,512]{2,1,0:T(8,128)} %broadcast_in_dim.9), calls=%async_computation.3 | async-start | bytes 2097152 | tf_op jit(solution)/shard_map/all_to_all | solution.py:246
  164.2 22.1 %collective-permute-start.30 = (f32[2,128,256]{2,1,0:T(8,128)S(1)}, f32[2,128,256]{2,1,0:T(8,128)S(1)}, u32[]{:S(2)}, u32[]{:S(2)}) collective-permute-start(f32[2,128,256]{2,1,0:T(8,128)S(1)} %get-tuple-element.54), channel_id=1, source_target_pairs={{0,8},{1,9},{2,10},{3,11},{4,12},{5,13},{6,14},{7,15},{8,0},{9,1},... | collective-permute-start | bytes 786440 | tf_op jit(solution)/shard_map/ppermute | solution.py:39
  165.3 21.0 %collective-permute-start.31 = (f32[2,128,256]{2,1,0:T(8,128)S(1)}, f32[2,128,256]{2,1,0:T(8,128)S(1)}, u32[]{:S(2)}, u32[]{:S(2)}) collective-permute-start(f32[2,128,256]{2,1,0:T(8,128)S(1)} %get-tuple-element.56), channel_id=1, source_target_pairs={{0,2},{1,3},{2,4},{3,5},{4,6},{5,7},{6,0},{7,1},{8,10},{9,11},{10,... | collective-permute-start | bytes 786440 | tf_op jit(solution)/shard_map/ppermute | solution.py:31
  166.5 19.8 %collective-permute-start.32 = (f32[2,128,256]{2,1,0:T(8,128)S(1)}, f32[2,128,256]{2,1,0:T(8,128)S(1)}, u32[]{:S(2)}, u32[]{:S(2)}) collective-permute-start(f32[2,128,256]{2,1,0:T(8,128)S(1)} %get-tuple-element.57), channel_id=1, source_target_pairs={{0,6},{1,7},{2,0},{3,1},{4,2},{5,3},{6,4},{7,5},{8,14},{9,15},{10,... | collective-permute-start | bytes 786440 | tf_op jit(solution)/shard_map/ppermute | solution.py:31
  168.0 20.0 %collective-permute-start.33 = (f32[2,128,256]{2,1,0:T(8,128)S(1)}, f32[2,128,256]{2,1,0:T(8,128)}, u32[]{:S(2)}, u32[]{:S(2)}) collective-permute-start(f32[2,128,256]{2,1,0:T(8,128)S(1)} %get-tuple-element.58), channel_id=1, source_target_pairs={{0,4},{1,5},{2,6},{3,7},{4,0},{5,1},{6,2},{7,3},{8,12},{9,13},{10,... | collective-permute-start | bytes 786440 | tf_op jit(solution)/shard_map/ppermute | solution.py:31
  180.8 13.3 %collective-permute-start.35 = (f32[512,512]{1,0:T(8,128)S(1)}, f32[512,512]{1,0:T(8,128)S(1)}, u32[]{:S(2)}, u32[]{:S(2)}) collective-permute-start(f32[512,512]{1,0:T(8,128)S(1)} %bitcast.50), channel_id=1, source_target_pairs={{0,1},{1,0},{2,3},{3,2},{4,5},{5,4},{6,7},{7,6},{8,9},{9,8},{10,11... | collective-permute-start | bytes 3145736 | tf_op jit(solution)/shard_map/ppermute | solution.py:27
  (9 other events, 106.7 us)
